TPU v7x, 32 devices: a whole 2x2x4 slice. The times are simulated.
32 devices in a mesh: cfg: 2 (over y), space: 4 (over z), tm: 4 (over x, core).
Axes of the slice: x: 2, y: 2, z: 4, core: 2. Of those that a mesh axis runs over, the one named last changes fastest.
Arguments:
- eigenvectors: bfloat16 [8, 2, 3, 3072, 384], P(('cfg', 'tm'), None, None, 'space'), parts along dimension 0, may hold values from -6 to 6
- perambulator: bfloat16 [8, 2, 1536, 1536], P(('cfg', 'tm'), None, None, 'space'), parts along dimension 0, may hold values from -0.3125 to 0.3125
- momenta: int32 [2, 3], replicated, may hold values from -2 to 2
- ratios: int32 [2, 2], replicated, may hold values from 1 to 3
- source_slice: int32 [1], replicated, may hold values from 0 to 255
Outputs:
- meson_blocks: float32 [8, 2, 1536, 1536], P(('cfg', 'tm'), None, 'space'), parts along dimension 0
There are 2 independent parts, one for each index of `cfg`. A program takes and returns all parts, laid end to end along the dimension named above; an argument that names none is the same for every part. Nothing has to cross between parts.
Inputs may be any that keep to these rules, and one draw needn't show every extreme that they name: `momenta`: row k is momentum k in units of 2 pi / 64. `ratios`: row k holds the numerator (column 0) and the denominator (column 1) of momentum k's coefficient.
All inputs are finite; a program needn't handle non-finite values.
Results may differ from a plain program's by a relative error of at most 0.0063.
Values may be sent and summed in bfloat16 or wider, within the bound.
No kernel may reach another device: no remote copies, remote signals or barrier semaphores. Data moves between devices by JAX's collectives and lax.ppermute only.
A program may use at most 64 MiB of HBM per device.

v0:
```python
import math

import jax
import jax.numpy as jnp
from jax import lax
from jax.experimental import pallas as pl
from jax.experimental.pallas import tpu as pltpu
from jax.sharding import PartitionSpec as P


LSIDE = 64
SPINS = 4


def spread(value, axis, source):
    kept = jnp.where(lax.axis_index(axis) == source, value, 0).astype(value.dtype)
    return lax.psum(kept, axis)


def site_phases(momenta, first_site, site_count):
    site_index = first_site + lax.iota(jnp.int32, site_count)
    along_x = site_index % LSIDE
    along_y = site_index // LSIDE % LSIDE
    along_z = site_index // (LSIDE * LSIDE)
    turn_count = (
        momenta[:, 0:1] * along_x[None, :]
        + momenta[:, 1:2] * along_y[None, :]
        + momenta[:, 2:3] * along_z[None, :]
    )
    phase_angle = (turn_count % LSIDE).astype(jnp.float32) * (2.0 * math.pi / LSIDE)
    return (jnp.cos(phase_angle), jnp.sin(phase_angle))


def split_elementals(product, vector_count):
    lead_shape = product.shape[:-2]
    product_grid = product.reshape(lead_shape + (2, vector_count, 2, 2, vector_count))
    real_part = product_grid[..., 0, :, :, 0, :] + product_grid[..., 1, :, :, 1, :]
    imaginary = product_grid[..., 0, :, :, 1, :] - product_grid[..., 1, :, :, 0, :]
    stacked = jnp.stack([real_part, imaginary], axis=-4)
    return jnp.moveaxis(stacked, -2, -4)


def elementals(vectors, cosine, sine_part):
    slab_count, color_count, site_count, vector_count = (
        vectors.shape[0],
        vectors.shape[2],
        vectors.shape[3],
        vectors.shape[4],
    )
    row_count = color_count * site_count
    real_rows = vectors[:, 0].reshape(slab_count, row_count, vector_count)
    imaginary_rows = vectors[:, 1].reshape(slab_count, row_count, vector_count)
    cos_rows = jnp.broadcast_to(cosine[:, None, :], (2, color_count, site_count)).reshape(
        1, 2, row_count, 1
    )
    sin_rows = jnp.broadcast_to(sine_part[:, None, :], (2, color_count, site_count)).reshape(
        1, 2, row_count, 1
    )
    phased_real = (cos_rows * real_rows[:, None] + sin_rows * imaginary_rows[:, None]).astype(
        jnp.bfloat16
    )
    phased_imaginary = (cos_rows * imaginary_rows[:, None] - sin_rows * real_rows[:, None]).astype(
        jnp.bfloat16
    )
    phased = jnp.concatenate([phased_real, phased_imaginary], axis=3)
    phased = jnp.transpose(phased, (0, 2, 1, 3)).reshape(slab_count, row_count, 4 * vector_count)
    plain_vectors = jnp.concatenate([real_rows, imaginary_rows], axis=2)
    product = lax.dot_general(
        plain_vectors, phased, (((1,), (1,)), ((0,), (0,))), preferred_element_type=jnp.float32
    )
    return split_elementals(product, vector_count)


def source_block(chosen):
    real_t = chosen[0].T
    imaginary_t = chosen[1].T
    upper = jnp.concatenate([real_t, -imaginary_t], axis=1)
    lower = jnp.concatenate([imaginary_t, real_t], axis=1)
    return jnp.concatenate([upper, lower], axis=0)


def propagate(sink_matrix, tau):
    vector_count = sink_matrix.shape[1]
    spin_count = tau.shape[1] // vector_count
    column_count = tau.shape[2]
    real_part, imaginary = (sink_matrix[0], sink_matrix[1])
    upper = jnp.concatenate([real_part, -imaginary], axis=1)
    lower = jnp.concatenate([imaginary, real_part], axis=1)
    sink_big = jnp.concatenate([upper, lower], axis=0)
    stacked = jnp.transpose(tau.reshape(2, spin_count, vector_count, column_count), (0, 2, 1, 3))
    stacked = stacked.reshape(2 * vector_count, spin_count * column_count)
    product = jnp.dot(sink_big, stacked, preferred_element_type=jnp.float32)
    product = jnp.transpose(
        product.reshape(2, vector_count, spin_count, column_count), (0, 2, 1, 3)
    )
    return product.reshape(2, spin_count * vector_count, column_count).astype(jnp.bfloat16)


def attach_source(propagated, source_big):
    vector_count = source_big.shape[0] // 2
    row_count = propagated.shape[1]
    spin_count = propagated.shape[2] // vector_count
    stacked = jnp.concatenate(
        [
            propagated[0].reshape(row_count, spin_count, vector_count),
            propagated[1].reshape(row_count, spin_count, vector_count),
        ],
        axis=2,
    )
    product = jnp.dot(
        stacked.reshape(row_count * spin_count, 2 * vector_count),
        source_big,
        preferred_element_type=jnp.float32,
    )
    product = jnp.transpose(product.reshape(row_count, spin_count, 2, vector_count), (2, 0, 1, 3))
    return product.reshape(2, row_count, spin_count * vector_count)


def general_body(eigenvectors, perambulator, momenta, ratios, source_slice):
    slab_count = eigenvectors.shape[0]
    color_count = eigenvectors.shape[2]
    site_count = eigenvectors.shape[3]
    vector_count = eigenvectors.shape[4]
    first_site = lax.axis_index("space") * site_count
    cosine, sine_part = site_phases(momenta, first_site, site_count)
    normalizer = 1.0 / math.sqrt(color_count * site_count * lax.axis_size("space") * vector_count)
    weights = (
        ratios[:, 0].astype(jnp.float32) / ratios[:, 1].astype(jnp.float32) * normalizer
    ).reshape(1, 2, 1, 1, 1)
    parts = elementals(eigenvectors, cosine, sine_part)
    partial_sums = jnp.sum(weights * parts, axis=1, keepdims=True)
    summed = lax.psum(partial_sums, "space")
    sink_matrices = summed[:, 0].astype(jnp.bfloat16)
    global_slice = source_slice[0] % (slab_count * lax.axis_size("tm"))
    local_source = lax.dynamic_index_in_dim(
        sink_matrices, global_slice % slab_count, 0, keepdims=False
    )
    chosen = spread(local_source, "tm", global_slice // slab_count)
    source_big = source_block(chosen)
    results = []
    for slab in range(slab_count):
        propagated = propagate(sink_matrices[slab], perambulator[slab])[None]
        turned = lax.all_to_all(propagated, "space", split_axis=2, concat_axis=3, tiled=True)
        results.append(attach_source(turned[0], source_big))
    return jnp.stack(results)


HBM = pl.BlockSpec(memory_space=pltpu.MemorySpace.HBM)


def in_hbm(array):
    return pltpu.with_memory_space_constraint(array, pltpu.MemorySpace.HBM)


def pick_kernel(tau_hbm, by3, by1, by2, buffer, in_sems, out_sems):
    place = lax.axis_index("space")
    loads = []
    stores = []
    for i, (r, out) in enumerate(((3, by3), (1, by1), (2, by2))):
        loads.append(pltpu.make_async_copy(tau_hbm.at[:, place ^ r], buffer.at[i], in_sems.at[i]))
        stores.append(pltpu.make_async_copy(buffer.at[i], out, out_sems.at[i]))
    for copy in loads:
        copy.start()
    for load, store in zip(loads, stores):
        load.wait()
        store.start()
    for copy in stores:
        copy.wait()


def pick_blocks(tau):
    _, _, n, columns = tau.shape
    return pl.pallas_call(
        pick_kernel,
        in_specs=[HBM],
        out_specs=[HBM] * 3,
        scratch_shapes=[
            pltpu.VMEM((3, 2, n, columns), tau.dtype),
            pltpu.SemaphoreType.DMA((3,)),
            pltpu.SemaphoreType.DMA((3,)),
        ],
        out_shape=[jax.ShapeDtypeStruct((2, n, columns), tau.dtype)] * 3,
        name="pick",
    )(in_hbm(tau))


def elemental_kernel(
    momenta_hbm,
    ratios_hbm,
    v_hbm,
    rounded_a,
    rounded_b,
    full_a,
    full_b,
    vectors,
    table,
    phased,
    total,
    momenta,
    ratios,
    sems,
    small_sems,
):
    place = lax.axis_index("space")
    colors = v_hbm.shape[1]
    site_count = v_hbm.shape[2]
    n = v_hbm.shape[3]
    half = n // 2
    loads = [
        pltpu.make_async_copy(v_hbm.at[:, c], vectors.at[c], sems.at[c]) for c in range(colors)
    ]
    small = [
        pltpu.make_async_copy(momenta_hbm, momenta, small_sems.at[0]),
        pltpu.make_async_copy(ratios_hbm, ratios, small_sems.at[1]),
    ]
    for copy in small + loads:
        copy.start()
    for copy in small:
        copy.wait()

    row = lax.broadcasted_iota(jnp.int32, (8, 128), 0)
    lane = lax.broadcasted_iota(jnp.int32, (8, 128), 1)
    second = (row & 1) == 1
    along = [jnp.where(second, momenta[1, a], momenta[0, a]) for a in range(3)]
    shift = jnp.where((row & 2) == 2, LSIDE - LSIDE // 4, 0)
    for tile in range(site_count // 128):
        site = place * site_count + tile * 128 + lane
        turn = (
            along[0] * (site % LSIDE)
            + along[1] * (site // LSIDE % LSIDE)
            + along[2] * (site // (LSIDE * LSIDE))
            + shift
        )
        turn = turn & (LSIDE - 1)
        angle = turn.astype(jnp.float32) * (2.0 * math.pi / LSIDE)
        table[pl.ds(tile * 128, 128), 0:8] = jnp.cos(angle).T

    def phase(color, k):
        slot = (2 * color + k) % 2
        real = vectors[color, 0].astype(jnp.float32)
        imag = vectors[color, 1].astype(jnp.float32)
        c = table[:, k : k + 1]
        s = table[:, k + 2 : k + 3]
        phased[slot, :, 0:n] = (c * real + s * imag).astype(jnp.bfloat16)
        phased[slot, :, n : 2 * n] = (c * imag - s * real).astype(jnp.bfloat16)

    def multiply(color, k):
        slot = (2 * color + k) % 2
        cols = slice(2 * k * n, (2 * k + 2) * n)
        for part in range(2):
            product = lax.dot_general(
                vectors[color, part],
                phased[slot],
                (((0,), (0,)), ((), ())),
                preferred_element_type=jnp.float32,
            )
            rows = slice(part * n, (part + 1) * n)
            if color == 0:
                total[rows, cols] = product
            else:
                total[rows, cols] += product

    before = None
    for color in range(colors):
        loads[color].wait()
        for k in range(2):
            phase(color, k)
            if before is not None:
                multiply(*before)
            before = (color, k)
    multiply(*before)

    normalizer = 1.0 / math.sqrt(colors * site_count * lax.axis_size("space") * n)
    re = 0.0
    im = 0.0
    for k in range(2):
        ratio = [jnp.full((8, 128), ratios[k, i], jnp.int32).astype(jnp.float32) for i in range(2)]
        w = (ratio[0] / ratio[1] * normalizer)[0:1, 0:1]
        zr = slice((2 * k) * n, (2 * k + 1) * n)
        zi = slice((2 * k + 1) * n, (2 * k + 2) * n)
        re += w * (total[0:n, zr] + total[n : 2 * n, zi])
        im += w * (total[0:n, zi] - total[n : 2 * n, zr])
    for part, value in enumerate((re, im)):
        small = value.astype(jnp.bfloat16)
        rounded_a[part] = small[:half]
        rounded_b[part] = small[half:]
        full_a[part] = value[:half]
        full_b[part] = value[half:]


def elemental_sums(vectors, momenta, ratios):
    _, color_count, site_count, n = vectors.shape
    half = n // 2
    rows = pl.BlockSpec((2, half, n), lambda i: (0, 0, 0))
    return pl.pallas_call(
        elemental_kernel,
        grid=(1,),
        in_specs=[HBM] * 3,
        out_specs=[rows] * 4,
        scratch_shapes=[
                pltpu.VMEM((color_count, 2, site_count, n), jnp.bfloat16),
                pltpu.VMEM((site_count, 128), jnp.float32),
                pltpu.VMEM((2, site_count, 2 * n), jnp.bfloat16),
                pltpu.VMEM((2 * n, 4 * n), jnp.float32),
                pltpu.SMEM(momenta.shape, jnp.int32),
                pltpu.SMEM(ratios.shape, jnp.int32),
                pltpu.SemaphoreType.DMA((color_count,)),
                pltpu.SemaphoreType.DMA((2,)),
        ],
        out_shape=[
            jax.ShapeDtypeStruct((2, half, n), dtype)
            for dtype in (jnp.bfloat16, jnp.bfloat16, jnp.float32, jnp.float32)
        ],
        compiler_params=pltpu.CompilerParams(vmem_limit_bytes=40 * 1024 * 1024),
        name="elementals",
    )(in_hbm(momenta), in_hbm(ratios), in_hbm(vectors))


def complex_rows(real, imag):
    upper = jnp.concatenate([real, imag], axis=1)
    lower = jnp.concatenate([-imag, real], axis=1)
    return jnp.concatenate([upper, lower], axis=0)


def sandwich(sink, tau_re, tau_im, source):
    prop = jnp.dot(sink, complex_rows(tau_re, tau_im), preferred_element_type=jnp.float32)
    return lax.dot_general(
        prop.astype(jnp.bfloat16),
        source,
        (((1,), (1,)), ((), ())),
        preferred_element_type=jnp.float32,
    )


def copy_if(flag, first, second, target, sem):
    @pl.when(flag == 1)
    def _():
        pltpu.make_async_copy(first, target, sem).start()

    @pl.when(flag != 1)
    def _():
        pltpu.make_async_copy(second, target, sem).start()


def is_inner(place):
    return jnp.where((place == 1) | (place == 2), 1, 0)


def three_kernel(source_slice, *refs):
    (sink_a, sink_b, here_a, here_b, far_a, far_b, beside_a, beside_b) = refs[:8]
    tau_hbm, got_n, got_a, got_c = refs[8:12]
    out_hbm, sink_out, source_out = refs[12:15]
    blocks, staged, block_sems, out_sems = refs[15:]
    n = sink_out.shape[0]
    place = lax.axis_index("space")
    time = lax.axis_index("tm")
    inner = is_inner(place)
    same = jnp.where(source_slice[0] % lax.axis_size("tm") // 2 == time // 2, 1, 0)
    odd = time % 2

    pltpu.make_async_copy(tau_hbm.at[:, place], blocks.at[0], block_sems.at[0]).start()
    pltpu.make_async_copy(got_n, blocks.at[1], block_sems.at[1]).start()
    copy_if(inner, got_a, got_c, blocks.at[2], block_sems.at[2])

    def halves(first, second):
        return jnp.concatenate([first, second], axis=0)

    sink = [halves(sink_a[part], sink_b[part]) for part in range(2)]
    sink_rows = jnp.concatenate(sink, axis=1)
    sink_out[...] = sink_rows

    def away(far, beside, part):
        upper = jnp.where(odd == 0, far[part], beside[part])
        lower = jnp.where(odd == 0, beside[part], far[part])
        return halves(upper, lower)

    source = [
        halves(
            *[
                jnp.where(same == 1, here[part], away(far, beside, part))
                for here, far, beside in ((here_a, far_a, beside_a), (here_b, far_b, beside_b))
            ]
        )
        for part in range(2)
    ]
    source_rows = complex_rows(*source)
    source_out[...] = source_rows

    stores = []
    for i in range(3):
        pltpu.make_async_copy(got_n, blocks.at[i], block_sems.at[i]).wait()
        product = sandwich(sink_rows, blocks[i, 0], blocks[i, 1], source_rows)
        staged[i, 0] = product[:, :n]
        staged[i, 1] = product[:, n:]
        partner = place ^ (i if i < 2 else 2 + inner)
        column = pl.multiple_of(partner * n, 128)
        store = pltpu.make_async_copy(
            staged.at[i], out_hbm.at[0, :, :, pl.ds(column, n)], out_sems.at[i]
        )
        store.start()
        stores.append(store)
    for store in stores:
        store.wait()


def three_blocks(source_slice, pieces, tau, got, spins):
    n = tau.shape[2]
    return pl.pallas_call(
        three_kernel,
        grid_spec=pltpu.PrefetchScalarGridSpec(
            num_scalar_prefetch=1,
            grid=(1,),
            in_specs=[pl.BlockSpec(piece.shape, lambda i, *_: (0, 0, 0)) for piece in pieces]
            + [HBM] * 4,
            out_specs=[
                HBM,
                pl.BlockSpec((n, 2 * n), lambda i, *_: (0, 0)),
                pl.BlockSpec((2 * n, 2 * n), lambda i, *_: (0, 0)),
            ],
            scratch_shapes=[
                pltpu.VMEM((3, 2, n, n), jnp.bfloat16),
                pltpu.VMEM((3, 2, n, n), jnp.float32),
                pltpu.SemaphoreType.DMA((3,)),
                pltpu.SemaphoreType.DMA((3,)),
            ],
        ),
        out_shape=[
            jax.ShapeDtypeStruct((1, 2, n, spins * n), jnp.float32),
            jax.ShapeDtypeStruct((n, 2 * n), jnp.bfloat16),
            jax.ShapeDtypeStruct((2 * n, 2 * n), jnp.bfloat16),
        ],
        compiler_params=pltpu.CompilerParams(vmem_limit_bytes=40 * 1024 * 1024),
        name="three",
    )(source_slice, *pieces, tau, *got)


def last_kernel(sink, source, got_b, got_d, _, out_hbm, block, staged, sem, out_sem):
    n = sink.shape[0]
    place = lax.axis_index("space")
    inner = is_inner(place)
    copy_if(inner, got_b, got_d, block, sem)
    pltpu.make_async_copy(got_b, block, sem).wait()
    product = sandwich(sink[...], block[0], block[1], source[...])
    staged[0] = product[:, :n]
    staged[1] = product[:, n:]
    column = pl.multiple_of((place ^ (3 - inner)) * n, 128)
    store = pltpu.make_async_copy(staged, out_hbm.at[0, :, :, pl.ds(column, n)], out_sem)
    store.start()
    store.wait()


def last_block(sink, source, got_b, got_d, out):
    n = sink.shape[0]
    return pl.pallas_call(
        last_kernel,
        grid=(1,),
        in_specs=[
            pl.BlockSpec((n, 2 * n), lambda i: (0, 0)),
            pl.BlockSpec((2 * n, 2 * n), lambda i: (0, 0)),
            HBM,
            HBM,
            HBM,
        ],
        out_specs=HBM,
        scratch_shapes=[
            pltpu.VMEM((2, n, n), jnp.bfloat16),
            pltpu.VMEM((2, n, n), jnp.float32),
            pltpu.SemaphoreType.DMA,
            pltpu.SemaphoreType.DMA,
        ],
        out_shape=jax.ShapeDtypeStruct(out.shape, out.dtype),
        input_output_aliases={4: 0},
        compiler_params=pltpu.CompilerParams(vmem_limit_bytes=40 * 1024 * 1024),
        name="last",
    )(sink, source, got_b, got_d, out)


def block_body(eigenvectors, perambulator, momenta, ratios, source_slice):
    return ordered_body(eigenvectors, perambulator, momenta, ratios, source_slice)


def ordered_body(eigenvectors, perambulator, momenta, ratios, source_slice):
    n = eigenvectors.shape[4]
    quarter = n // 4
    spins = lax.axis_size("space")
    j = lax.axis_index("space")
    inner = (j == 1) | (j == 2)
    odd = lax.axis_index("tm") % 2
    tau = perambulator[0].reshape(2, spins, n, n)

    def move(value, pairs, axis="space"):
        return lax.ppermute(value, axis, pairs)

    middle = [(1, 2), (2, 1)]
    ends = [(0, 3), (3, 0)]
    inward = [(0, 1), (3, 2)]
    outward = [(1, 0), (2, 3)]
    skip_in = [(0, 2), (3, 1)]
    skip_out = [(1, 3), (2, 0)]
    core = [(0, 1), (1, 0), (2, 3), (3, 2)]
    chip = [(0, 2), (2, 0), (1, 3), (3, 1)]

    by3, by1, by2 = pick_blocks(tau)
    got_a = move(by3, middle)
    got_n = move(by1, inward + outward)
    got_c = move(by2, skip_out)
    rounded_a, rounded_b, full_a, full_b = elemental_sums(eigenvectors[0], momenta, ratios)
    got_b = move(by2, skip_in)
    got_d = move(by3, ends)

    pieces = []
    for rounded, full in ((rounded_a, full_a), (rounded_b, full_b)):
        inside = move(rounded, inward)
        pair = full + inside.astype(jnp.float32)
        across = move(pair.astype(jnp.bfloat16), middle)
        summed = (pair + across.astype(jnp.float32)).astype(jnp.bfloat16)
        outside = move(summed, outward)
        sink = jnp.where(inner, summed, outside)
        partner = move(sink, core, "tm")
        here = jnp.where(source_slice[0] % 2 == odd, sink, partner)
        mine = lax.dynamic_slice_in_dim(here, odd * quarter, quarter, 1)
        far = move(mine, chip, "tm")
        beside = move(far, core, "tm")
        pieces.append((sink, here, far, beside))
    pieces = [piece for pair in zip(*pieces) for piece in pair]

    out, sink, source = three_blocks(source_slice, pieces, tau, (got_n, got_a, got_c), spins)
    return last_block(sink, source, got_b, got_d, out)


def fits(mesh, eigenvectors, perambulator):
    n = eigenvectors.shape[4]
    space = mesh.shape["space"]
    return (
        eigenvectors.shape[0] == mesh.shape["cfg"] * mesh.shape["tm"]
        and space == SPINS
        and mesh.shape["tm"] == 4
        and perambulator.shape[2] == space * n
        and perambulator.shape[3] == space * n
        and eigenvectors.shape[3] % (128 * space) == 0
        and n % 128 == 0
    )


def solution(mesh):
    placed = (
        P(("cfg", "tm"), None, None, "space", None),
        P(("cfg", "tm"), None, None, "space"),
        P(),
        P(),
        P(),
    )

    def mapped(body):
        return jax.shard_map(
            body,
            mesh=mesh,
            in_specs=placed,
            out_specs=P(("cfg", "tm"), None, "space", None),
            check_vma=False,
        )

    def program(*arrays):
        if not fits(mesh, arrays[0], arrays[1]):
            return mapped(general_body)(*arrays)
        return mapped(block_body)(*arrays)

    return program
```

profile of v0, /device:TPU:0, one launch (start us, length us, event | category | flops | bytes accessed | tf_op | source)
XLA Modules:
  0.0 111.3 jit_solution(8801974611182324441)
XLA Ops:
  0.0 8.2 %elementals.1 = (bf16[2,192,384]{2,1,0:T(8,128)(2,1)S(1)}, bf16[2,192,384]{2,1,0:T(8,128)(2,1)S(1)}, f32[2,192,384]{2,1,0:T(8,128)S(1)}, f32[2,192,384]{2,1,0:T(8,128)S(1)}) custom-call(s32[2,3]{1,0:T(2,128)} %momenta_hbm.1, s32[2,2]{1,0:T(2,128)} %ratios_hbm.1, bf16[2,3,768,384]{3,2,1,0:T(8,128)(2,1)} %bitcast.8), custom_call_target="tpu_custom_call" | custom-call | tf_op jit(solution)/shard_map/elementals/pallas_call | solution.py:295
  8.2 5.0 %collective-permute-start = (bf16[2,192,384]{2,1,0:T(8,128)(2,1)S(1)}, bf16[2,192,384]{2,1,0:T(8,128)(2,1)S(1)}, u32[]{:S(2)}, u32[]{:S(2)}) collective-permute-start(bf16[2,192,384]{2,1,0:T(8,128)(2,1)S(1)} %get-tuple-element.16), channel_id=1, source_target_pairs={{0,4},{12,8},{1,5},{13,9},{2,6},{14,10},{3,7},{15,11},{16,20},{28,... | collective-permute-start | bytes 884744 | tf_op jit(solution)/shard_map/ppermute | solution.py:492
  13.2 1.3 %collective-permute-start.3 = (bf16[2,192,384]{2,1,0:T(8,128)(2,1)S(1)}, bf16[2,192,384]{2,1,0:T(8,128)(2,1)S(1)}, u32[]{:S(2)}, u32[]{:S(2)}) collective-permute-start(bf16[2,192,384]{2,1,0:T(8,128)(2,1)S(1)} %get-tuple-element.18), channel_id=1, source_target_pairs={{0,4},{12,8},{1,5},{13,9},{2,6},{14,10},{3,7},{15,11},{16,20},{28,... | collective-permute-start | bytes 884744 | tf_op jit(solution)/shard_map/ppermute | solution.py:492
  14.5 6.0 %collective-permute-done = bf16[2,192,384]{2,1,0:T(8,128)(2,1)S(1)} collective-permute-done((bf16[2,192,384]{2,1,0:T(8,128)(2,1)S(1)}, bf16[2,192,384]{2,1,0:T(8,128)(2,1)S(1)}, u32[]{:S(2)}, u32[]{:S(2)}) %collective-permute-start) | collective-permute-done | bytes 294944 | tf_op jit(solution)/shard_map/ppermute | solution.py:492
  20.6 0.1 fusion
  20.6 0.7 collective-permute-start.1
  21.3 4.4 %collective-permute-done.3 = bf16[2,192,384]{2,1,0:T(8,128)(2,1)S(1)} collective-permute-done((bf16[2,192,384]{2,1,0:T(8,128)(2,1)S(1)}, bf16[2,192,384]{2,1,0:T(8,128)(2,1)S(1)}, u32[]{:S(2)}, u32[]{:S(2)}) %collective-permute-start.3) | collective-permute-done | bytes 294944 | tf_op jit(solution)/shard_map/ppermute | solution.py:492
  25.8 0.1 fusion.1
  25.8 0.7 collective-permute-start.4
  26.5 0.1 add_convert_fusion.1
  26.6 1.3 %collective-permute-start.2 = (bf16[2,192,384]{2,1,0:T(8,128)(2,1)S(1)}, bf16[2,192,384]{2,1,0:T(8,128)(2,1)S(1)}, u32[]{:S(2)}, u32[]{:S(2)}) collective-permute-start(bf16[2,192,384]{2,1,0:T(8,128)(2,1)S(1)} %add_convert_fusion.1), channel_id=1, source_target_pairs={{4,0},{8,12},{5,1},{9,13},{6,2},{10,14},{7,3},{11,15},{20,16},{24,... | collective-permute-start | bytes 884744 | tf_op jit(solution)/shard_map/ppermute | solution.py:492
  27.9 0.1 add_convert_fusion
  28.1 1.4 %collective-permute-start.5 = (bf16[2,192,384]{2,1,0:T(8,128)(2,1)S(1)}, bf16[2,192,384]{2,1,0:T(8,128)(2,1)}, u32[]{:S(2)}, u32[]{:S(2)}) collective-permute-start(bf16[2,192,384]{2,1,0:T(8,128)(2,1)S(1)} %add_convert_fusion), channel_id=1, source_target_pairs={{4,0},{8,12},{5,1},{9,13},{6,2},{10,14},{7,3},{11,15},{20,16},{24,... | collective-permute-start | bytes 884744 | tf_op jit(solution)/shard_map/ppermute | solution.py:492
  29.5 10.0 %collective-permute-done.2 = bf16[2,192,384]{2,1,0:T(8,128)(2,1)S(1)} collective-permute-done((bf16[2,192,384]{2,1,0:T(8,128)(2,1)S(1)}, bf16[2,192,384]{2,1,0:T(8,128)(2,1)S(1)}, u32[]{:S(2)}, u32[]{:S(2)}) %collective-permute-start.2) | collective-permute-done | bytes 294944 | tf_op jit(solution)/shard_map/ppermute | solution.py:492
  39.6 0.1 collective-permute-start.6
  39.7 5.8 %collective-permute-done.5 = bf16[2,192,384]{2,1,0:T(8,128)(2,1)} collective-permute-done((bf16[2,192,384]{2,1,0:T(8,128)(2,1)S(1)}, bf16[2,192,384]{2,1,0:T(8,128)(2,1)}, u32[]{:S(2)}, u32[]{:S(2)}) %collective-permute-start.5) | collective-permute-done | bytes 294944 | tf_op jit(solution)/shard_map/ppermute | solution.py:492
  45.5 1.0 broadcast_select_fusion.2.refs_1_
  46.5 0.1 collective-permute-start.7
  46.6 2.4 %pick.1 = (bf16[2,384,384]{2,1,0:T(8,128)(2,1)}, bf16[2,384,384]{2,1,0:T(8,128)(2,1)}, bf16[2,384,384]{2,1,0:T(8,128)(2,1)}) custom-call(bf16[2,4,384,384]{3,2,1,0:T(8,128)(2,1)} %bitcast.6), custom_call_target="tpu_custom_call" | custom-call | tf_op jit(solution)/shard_map/pick/pallas_call | solution.py:173
  48.9 3.9 %collective-permute-start.16 = (bf16[2,384,384]{2,1,0:T(8,128)(2,1)}, bf16[2,384,384]{2,1,0:T(8,128)(2,1)S(1)}, u32[]{:S(2)}, u32[]{:S(2)}) collective-permute-start(bf16[2,384,384]{2,1,0:T(8,128)(2,1)} %get-tuple-element.20), channel_id=1, source_target_pairs={{0,12},{12,0},{1,13},{13,1},{2,14},{14,2},{3,15},{15,3},{16,28},{2... | collective-permute-start | bytes 1769480 | tf_op jit(solution)/shard_map/ppermute | solution.py:492
  52.9 1.5 %collective-permute-start.13 = (bf16[2,384,384]{2,1,0:T(8,128)(2,1)}, bf16[2,384,384]{2,1,0:T(8,128)(2,1)}, u32[]{:S(2)}, u32[]{:S(2)}) collective-permute-start(bf16[2,384,384]{2,1,0:T(8,128)(2,1)} %get-tuple-element.20), channel_id=1, source_target_pairs={{4,8},{8,4},{5,9},{9,5},{6,10},{10,6},{7,11},{11,7},{20,24},{24,20... | collective-permute-start | bytes 1769480 | tf_op jit(solution)/shard_map/ppermute | solution.py:492
  55.0 4.3 %collective-permute-start.15 = (bf16[2,384,384]{2,1,0:T(8,128)(2,1)}, bf16[2,384,384]{2,1,0:T(8,128)(2,1)S(1)}, u32[]{:S(2)}, u32[]{:S(2)}) collective-permute-start(bf16[2,384,384]{2,1,0:T(8,128)(2,1)} %get-tuple-element.21), channel_id=1, source_target_pairs={{0,8},{12,4},{1,9},{13,5},{2,10},{14,6},{3,11},{15,7},{16,24},{28,... | collective-permute-start | bytes 1769480 | tf_op jit(solution)/shard_map/ppermute | solution.py:492
  59.4 0.1 broadcast_select_fusion.1.refs_2_
  59.4 1.3 %collective-permute-start.14 = (bf16[2,384,384]{2,1,0:T(8,128)(2,1)}, bf16[2,384,384]{2,1,0:T(8,128)(2,1)S(1)}, u32[]{:S(2)}, u32[]{:S(2)}) collective-permute-start(bf16[2,384,384]{2,1,0:T(8,128)(2,1)} %get-tuple-element.21), channel_id=1, source_target_pairs={{4,12},{8,0},{5,13},{9,1},{6,14},{10,2},{7,15},{11,3},{20,28},{24,... | collective-permute-start | bytes 1769480 | tf_op jit(solution)/shard_map/ppermute | solution.py:492
  60.9 23.9 %collective-permute-done.12.refs_9_ = bf16[2,384,384]{2,1,0:T(8,128)(2,1)} collective-permute-done((bf16[2,384,384]{2,1,0:T(8,128)(2,1)}, bf16[2,384,384]{2,1,0:T(8,128)(2,1)}, u32[]{:S(2)}, u32[]{:S(2)}) %collective-permute-start.12) | collective-permute-done | bytes 589856 | tf_op jit(solution)/shard_map/ppermute | solution.py:492
  84.7 1.5 %collective-permute-start.8 = (bf16[2,96,384]{2,1,0:T(8,128)(2,1)S(1)}, bf16[2,96,384]{2,1,0:T(8,128)(2,1)S(1)}, u32[]{:S(2)}, u32[]{:S(2)}) collective-permute-start(bf16[2,96,384]{2,1,0:T(8,128)(2,1)S(1)} %constant_dynamic-slice_fusion.1), channel_id=1, source_target_pairs={{0,2},{2,0},{1,3},{3,1},{4,6},{6,4},{5,7},{7,5},{8,10},{10,8},{9,1... | collective-permute-start | bytes 442376 | tf_op jit(solution)/shard_map/ppermute | solution.py:492
  86.2 0.5 collective-permute-start.9
  86.8 4.7 %collective-permute-done.8.refs_4_ = bf16[2,96,384]{2,1,0:T(8,128)(2,1)S(1)} collective-permute-done((bf16[2,96,384]{2,1,0:T(8,128)(2,1)S(1)}, bf16[2,96,384]{2,1,0:T(8,128)(2,1)S(1)}, u32[]{:S(2)}, u32[]{:S(2)}) %collective-permute-start.8) | collective-permute-done | bytes 147488 | tf_op jit(solution)/shard_map/ppermute | solution.py:492
  91.5 2.2 %collective-permute-done.9.refs_5_ = bf16[2,96,384]{2,1,0:T(8,128)(2,1)S(1)} collective-permute-done((bf16[2,96,384]{2,1,0:T(8,128)(2,1)S(1)}, bf16[2,96,384]{2,1,0:T(8,128)(2,1)S(1)}, u32[]{:S(2)}, u32[]{:S(2)}) %collective-permute-start.9) | collective-permute-done | bytes 147488 | tf_op jit(solution)/shard_map/ppermute | solution.py:492
  93.7 9.7 %collective-permute-done.14.refs_11_ = bf16[2,384,384]{2,1,0:T(8,128)(2,1)S(1)} collective-permute-done((bf16[2,384,384]{2,1,0:T(8,128)(2,1)}, bf16[2,384,384]{2,1,0:T(8,128)(2,1)S(1)}, u32[]{:S(2)}, u32[]{:S(2)}) %collective-permute-start.14) | collective-permute-done | bytes 589856 | tf_op jit(solution)/shard_map/ppermute | solution.py:492
  103.4 5.4 %three.1 = (f32[1,2,384,1536]{3,2,1,0:T(8,128)}, bf16[384,768]{1,0:T(8,128)(2,1)S(1)}, bf16[768,768]{1,0:T(8,128)(2,1)S(1)}) custom-call(s32[1]{0:T(128)} %copy.8.source_slice, bf16[2,192,384]{2,1,0:T(8,128)(2,1)S(1)} %broadcast_select_fusion.3.refs_0_, bf16[2,192,384]{2,1,0:T(8,128)(2,1)S(1)} %broadcast_select_fusion.2.refs_1_, ...), custom_call_target="tpu_custom_call" | custom-call | tf_op jit(solution)/shard_map/three/pallas_call | solution.py:408
  108.8 2.4 %last.1 = f32[1,2,384,1536]{3,2,1,0:T(8,128)} custom-call(bf16[384,768]{1,0:T(8,128)(2,1)S(1)} %get-tuple-element.22.sink, bf16[768,768]{1,0:T(8,128)(2,1)S(1)} %get-tuple-element.23.source, bf16[2,384,384]{2,1,0:T(8,128)(2,1)S(1)} %collective-permute-done.15.got_b, ...), custom_call_target="tpu_custom_call", output_to_operand_aliasing={{}: (4, {})} | custom-call | tf_op jit(solution)/shard_map/last/pallas_call | solution.py:454
  (18 shorter events, 0.2 us)
Async XLA Ops:
  8.2 12.3 %collective-permute-start = (bf16[2,192,384]{2,1,0:T(8,128)(2,1)S(1)}, bf16[2,192,384]{2,1,0:T(8,128)(2,1)S(1)}, u32[]{:S(2)}, u32[]{:S(2)}) collective-permute-start(bf16[2,192,384]{2,1,0:T(8,128)(2,1)S(1)} %get-tuple-element.16), channel_id=1, source_target_pairs={{0,4},{12,8},{1,5},{13,9},{2,6},{14,10},{3,7},{15,11},{16,20},{28,... | collective-permute-start | bytes 884744 | tf_op jit(solution)/shard_map/ppermute | solution.py:492
  13.2 12.6 %collective-permute-start.3 = (bf16[2,192,384]{2,1,0:T(8,128)(2,1)S(1)}, bf16[2,192,384]{2,1,0:T(8,128)(2,1)S(1)}, u32[]{:S(2)}, u32[]{:S(2)}) collective-permute-start(bf16[2,192,384]{2,1,0:T(8,128)(2,1)S(1)} %get-tuple-element.18), channel_id=1, source_target_pairs={{0,4},{12,8},{1,5},{13,9},{2,6},{14,10},{3,7},{15,11},{16,20},{28,... | collective-permute-start | bytes 884744 | tf_op jit(solution)/shard_map/ppermute | solution.py:492
  20.6 5.9 %collective-permute-start.1 = (bf16[2,192,384]{2,1,0:T(8,128)(2,1)S(1)}, bf16[2,192,384]{2,1,0:T(8,128)(2,1)S(1)}, u32[]{:S(2)}, u32[]{:S(2)}) collective-permute-start(bf16[2,192,384]{2,1,0:T(8,128)(2,1)S(1)} %fusion), channel_id=1, source_target_pairs={{4,8},{8,4},{5,9},{9,5},{6,10},{10,6},{7,11},{11,7},{20,24},{24,20... | collective-permute-start | bytes 884744 | tf_op jit(solution)/shard_map/ppermute | solution.py:492
  25.8 2.1 %collective-permute-start.4 = (bf16[2,192,384]{2,1,0:T(8,128)(2,1)S(1)}, bf16[2,192,384]{2,1,0:T(8,128)(2,1)S(1)}, u32[]{:S(2)}, u32[]{:S(2)}) collective-permute-start(bf16[2,192,384]{2,1,0:T(8,128)(2,1)S(1)} %fusion.1), channel_id=1, source_target_pairs={{4,8},{8,4},{5,9},{9,5},{6,10},{10,6},{7,11},{11,7},{20,24},{24,20... | collective-permute-start | bytes 884744 | tf_op jit(solution)/shard_map/ppermute | solution.py:492
  26.6 12.9 %collective-permute-start.2 = (bf16[2,192,384]{2,1,0:T(8,128)(2,1)S(1)}, bf16[2,192,384]{2,1,0:T(8,128)(2,1)S(1)}, u32[]{:S(2)}, u32[]{:S(2)}) collective-permute-start(bf16[2,192,384]{2,1,0:T(8,128)(2,1)S(1)} %add_convert_fusion.1), channel_id=1, source_target_pairs={{4,0},{8,12},{5,1},{9,13},{6,2},{10,14},{7,3},{11,15},{20,16},{24,... | collective-permute-start | bytes 884744 | tf_op jit(solution)/shard_map/ppermute | solution.py:492
  28.0 75.3 %copy-start = (bf16[1,2,1536,384]{3,2,1,0:T(8,128)(2,1)S(1)}, bf16[1,2,1536,384]{3,2,1,0:T(8,128)(2,1)}, u32[]{:S(2)}) copy-start(bf16[1,2,1536,384]{3,2,1,0:T(8,128)(2,1)} %param.6) | copy-start | bytes 7077892
  28.1 17.4 %collective-permute-start.5 = (bf16[2,192,384]{2,1,0:T(8,128)(2,1)S(1)}, bf16[2,192,384]{2,1,0:T(8,128)(2,1)}, u32[]{:S(2)}, u32[]{:S(2)}) collective-permute-start(bf16[2,192,384]{2,1,0:T(8,128)(2,1)S(1)} %add_convert_fusion), channel_id=1, source_target_pairs={{4,0},{8,12},{5,1},{9,13},{6,2},{10,14},{7,3},{11,15},{20,16},{24,... | collective-permute-start | bytes 884744 | tf_op jit(solution)/shard_map/ppermute | solution.py:492
  39.6 15.5 %collective-permute-start.6 = (bf16[2,192,384]{2,1,0:T(8,128)(2,1)S(1)}, bf16[2,192,384]{2,1,0:T(8,128)(2,1)}, u32[]{:S(2)}, u32[]{:S(2)}) collective-permute-start(bf16[2,192,384]{2,1,0:T(8,128)(2,1)S(1)} %broadcast_select_fusion.3.refs_0_), channel_id=1, source_target_pairs={{0,1},{1,0},{2,3},{3,2},{4,5},{5,4},{6,7},{7,6},{8,9},{9,8},{10,11... | collective-permute-start | bytes 884744 | tf_op jit(solution)/shard_map/ppermute | solution.py:492
  46.5 12.9 %collective-permute-start.7 = (bf16[2,192,384]{2,1,0:T(8,128)(2,1)S(1)}, bf16[2,192,384]{2,1,0:T(8,128)(2,1)}, u32[]{:S(2)}, u32[]{:S(2)}) collective-permute-start(bf16[2,192,384]{2,1,0:T(8,128)(2,1)S(1)} %broadcast_select_fusion.2.refs_1_), channel_id=1, source_target_pairs={{0,1},{1,0},{2,3},{3,2},{4,5},{5,4},{6,7},{7,6},{8,9},{9,8},{10,11... | collective-permute-start | bytes 884744 | tf_op jit(solution)/shard_map/ppermute | solution.py:492
  48.9 59.8 %collective-permute-start.16 = (bf16[2,384,384]{2,1,0:T(8,128)(2,1)}, bf16[2,384,384]{2,1,0:T(8,128)(2,1)S(1)}, u32[]{:S(2)}, u32[]{:S(2)}) collective-permute-start(bf16[2,384,384]{2,1,0:T(8,128)(2,1)} %get-tuple-element.20), channel_id=1, source_target_pairs={{0,12},{12,0},{1,13},{13,1},{2,14},{14,2},{3,15},{15,3},{16,28},{2... | collective-permute-start | bytes 1769480 | tf_op jit(solution)/shard_map/ppermute | solution.py:492
  52.9 33.4 %collective-permute-start.13 = (bf16[2,384,384]{2,1,0:T(8,128)(2,1)}, bf16[2,384,384]{2,1,0:T(8,128)(2,1)}, u32[]{:S(2)}, u32[]{:S(2)}) collective-permute-start(bf16[2,384,384]{2,1,0:T(8,128)(2,1)} %get-tuple-element.20), channel_id=1, source_target_pairs={{4,8},{8,4},{5,9},{9,5},{6,10},{10,6},{7,11},{11,7},{20,24},{24,20... | collective-permute-start | bytes 1769480 | tf_op jit(solution)/shard_map/ppermute | solution.py:492
  54.4 30.4 %collective-permute-start.12 = (bf16[2,384,384]{2,1,0:T(8,128)(2,1)}, bf16[2,384,384]{2,1,0:T(8,128)(2,1)}, u32[]{:S(2)}, u32[]{:S(2)}) collective-permute-start(bf16[2,384,384]{2,1,0:T(8,128)(2,1)} %get-tuple-element.19), channel_id=1, source_target_pairs={{0,4},{12,8},{4,0},{8,12},{1,5},{13,9},{5,1},{9,13},{2,6},{14,10},... | collective-permute-start | bytes 1769480 | tf_op jit(solution)/shard_map/ppermute | solution.py:492
  55.0 53.7 %collective-permute-start.15 = (bf16[2,384,384]{2,1,0:T(8,128)(2,1)}, bf16[2,384,384]{2,1,0:T(8,128)(2,1)S(1)}, u32[]{:S(2)}, u32[]{:S(2)}) collective-permute-start(bf16[2,384,384]{2,1,0:T(8,128)(2,1)} %get-tuple-element.21), channel_id=1, source_target_pairs={{0,8},{12,4},{1,9},{13,5},{2,10},{14,6},{3,11},{15,7},{16,24},{28,... | collective-permute-start | bytes 1769480 | tf_op jit(solution)/shard_map/ppermute | solution.py:492
  59.4 43.9 %collective-permute-start.14 = (bf16[2,384,384]{2,1,0:T(8,128)(2,1)}, bf16[2,384,384]{2,1,0:T(8,128)(2,1)S(1)}, u32[]{:S(2)}, u32[]{:S(2)}) collective-permute-start(bf16[2,384,384]{2,1,0:T(8,128)(2,1)} %get-tuple-element.21), channel_id=1, source_target_pairs={{4,12},{8,0},{5,13},{9,1},{6,14},{10,2},{7,15},{11,3},{20,28},{24,... | collective-permute-start | bytes 1769480 | tf_op jit(solution)/shard_map/ppermute | solution.py:492
  84.7 6.7 %collective-permute-start.8 = (bf16[2,96,384]{2,1,0:T(8,128)(2,1)S(1)}, bf16[2,96,384]{2,1,0:T(8,128)(2,1)S(1)}, u32[]{:S(2)}, u32[]{:S(2)}) collective-permute-start(bf16[2,96,384]{2,1,0:T(8,128)(2,1)S(1)} %constant_dynamic-slice_fusion.1), channel_id=1, source_target_pairs={{0,2},{2,0},{1,3},{3,1},{4,6},{6,4},{5,7},{7,5},{8,10},{10,8},{9,1... | collective-permute-start | bytes 442376 | tf_op jit(solution)/shard_map/ppermute | solution.py:492
  86.2 7.5 %collective-permute-start.9 = (bf16[2,96,384]{2,1,0:T(8,128)(2,1)S(1)}, bf16[2,96,384]{2,1,0:T(8,128)(2,1)S(1)}, u32[]{:S(2)}, u32[]{:S(2)}) collective-permute-start(bf16[2,96,384]{2,1,0:T(8,128)(2,1)S(1)} %constant_dynamic-slice_fusion), channel_id=1, source_target_pairs={{0,2},{2,0},{1,3},{3,1},{4,6},{6,4},{5,7},{7,5},{8,10},{10,8},{9,1... | collective-permute-start | bytes 442376 | tf_op jit(solution)/shard_map/ppermute | solution.py:492
  91.5 11.9 %collective-permute-start.10 = (bf16[2,96,384]{2,1,0:T(8,128)(2,1)S(1)}, bf16[2,96,384]{2,1,0:T(8,128)(2,1)S(1)}, u32[]{:S(2)}, u32[]{:S(2)}) collective-permute-start(bf16[2,96,384]{2,1,0:T(8,128)(2,1)S(1)} %collective-permute-done.8.refs_4_), channel_id=1, source_target_pairs={{0,1},{1,0},{2,3},{3,2},{4,5},{5,4},{6,7},{7,6},{8,9},{9,8},{10,11... | collective-permute-start | bytes 442376 | tf_op jit(solution)/shard_map/ppermute | solution.py:492
  93.7 9.7 %collective-permute-start.11 = (bf16[2,96,384]{2,1,0:T(8,128)(2,1)S(1)}, bf16[2,96,384]{2,1,0:T(8,128)(2,1)S(1)}, u32[]{:S(2)}, u32[]{:S(2)}) collective-permute-start(bf16[2,96,384]{2,1,0:T(8,128)(2,1)S(1)} %collective-permute-done.9.refs_5_), channel_id=1, source_target_pairs={{0,1},{1,0},{2,3},{3,2},{4,5},{5,4},{6,7},{7,6},{8,9},{9,8},{10,11... | collective-permute-start | bytes 442376 | tf_op jit(solution)/shard_map/ppermute | solution.py:492
where the time goes:
time: 112 us; the launch traced here: 111 us
  waiting for transfers between devices  66.8 us (60%)
  starting transfers between devices  23.5 us (21%)
  Pallas kernels  18.4 us (16%)
  other arithmetic  1.45 us (1%)
    ppermute x17, waiting for transfers between devices, move(): return lax.ppermute(value, axis, pairs)  66.8 us
    ppermute x17, starting transfers between devices, move(): return lax.ppermute(value, axis, pairs)  23.5 us
    pallas_call x1, Pallas kernels, elemental_sums(): pl.pallas_call(elemental_kernel, grid=(1,), in_specs=[HBM] * 3, out_specs...  8.23 us
    pallas_call x1, Pallas kernels, three_blocks(): pl.pallas_call(three_kernel, grid_spec=pltpu.PrefetchScalarGridSpec(num_s...  5.39 us
    pallas_call x1, Pallas kernels, last_block(): pl.pallas_call(last_kernel, grid=(1,), in_specs=[pl.BlockSpec((n, 2 * n),...  2.38 us
    pallas_call x1, Pallas kernels, pick_blocks(): pl.pallas_call(pick_kernel, in_specs=[HBM], out_specs=[HBM] * 3, scratch_...  2.36 us
  transfers between devices with their start and end apart: 17, of which 8 were waited for; matrix products, arithmetic and copies ran while one was open for 1% of the time, Pallas kernels for 7%

commit v1 on v0

--- a/solution.py
+++ b/solution.py
@@ -332,35 +332,20 @@
     )
 
 
-def copy_if(flag, first, second, target, sem):
-    @pl.when(flag == 1)
-    def _():
-        pltpu.make_async_copy(first, target, sem).start()
-
-    @pl.when(flag != 1)
-    def _():
-        pltpu.make_async_copy(second, target, sem).start()
-
-
-def is_inner(place):
-    return jnp.where((place == 1) | (place == 2), 1, 0)
-
-
 def three_kernel(source_slice, *refs):
     (sink_a, sink_b, here_a, here_b, far_a, far_b, beside_a, beside_b) = refs[:8]
-    tau_hbm, got_n, got_a, got_c = refs[8:12]
-    out_hbm, sink_out, source_out = refs[12:15]
-    blocks, staged, block_sems, out_sems = refs[15:]
+    tau_hbm, got1, got3 = refs[8:11]
+    out_hbm, sink_out, source_out = refs[11:14]
+    blocks, staged, block_sems, out_sems = refs[14:]
     n = sink_out.shape[0]
     place = lax.axis_index("space")
     time = lax.axis_index("tm")
-    inner = is_inner(place)
     same = jnp.where(source_slice[0] % lax.axis_size("tm") // 2 == time // 2, 1, 0)
     odd = time % 2
 
     pltpu.make_async_copy(tau_hbm.at[:, place], blocks.at[0], block_sems.at[0]).start()
-    pltpu.make_async_copy(got_n, blocks.at[1], block_sems.at[1]).start()
-    copy_if(inner, got_a, got_c, blocks.at[2], block_sems.at[2])
+    pltpu.make_async_copy(got1, blocks.at[1], block_sems.at[1]).start()
+    pltpu.make_async_copy(got3, blocks.at[2], block_sems.at[2]).start()
 
     def halves(first, second):
         return jnp.concatenate([first, second], axis=0)
@@ -388,12 +373,11 @@
 
     stores = []
     for i in range(3):
-        pltpu.make_async_copy(got_n, blocks.at[i], block_sems.at[i]).wait()
+        pltpu.make_async_copy(got1, blocks.at[i], block_sems.at[i]).wait()
         product = sandwich(sink_rows, blocks[i, 0], blocks[i, 1], source_rows)
         staged[i, 0] = product[:, :n]
         staged[i, 1] = product[:, n:]
-        partner = place ^ (i if i < 2 else 2 + inner)
-        column = pl.multiple_of(partner * n, 128)
+        column = pl.multiple_of((place ^ (0, 1, 3)[i]) * n, 128)
         store = pltpu.make_async_copy(
             staged.at[i], out_hbm.at[0, :, :, pl.ds(column, n)], out_sems.at[i]
         )
@@ -411,7 +395,7 @@
             num_scalar_prefetch=1,
             grid=(1,),
             in_specs=[pl.BlockSpec(piece.shape, lambda i, *_: (0, 0, 0)) for piece in pieces]
-            + [HBM] * 4,
+            + [HBM] * 3,
             out_specs=[
                 HBM,
                 pl.BlockSpec((n, 2 * n), lambda i, *_: (0, 0)),
@@ -434,22 +418,22 @@
     )(source_slice, *pieces, tau, *got)
 
 
-def last_kernel(sink, source, got_b, got_d, _, out_hbm, block, staged, sem, out_sem):
+def last_kernel(sink, source, got2, _, out_hbm, block, staged, sem, out_sem):
     n = sink.shape[0]
     place = lax.axis_index("space")
-    inner = is_inner(place)
-    copy_if(inner, got_b, got_d, block, sem)
-    pltpu.make_async_copy(got_b, block, sem).wait()
+    load = pltpu.make_async_copy(got2, block, sem)
+    load.start()
+    load.wait()
     product = sandwich(sink[...], block[0], block[1], source[...])
     staged[0] = product[:, :n]
     staged[1] = product[:, n:]
-    column = pl.multiple_of((place ^ (3 - inner)) * n, 128)
+    column = pl.multiple_of((place ^ 2) * n, 128)
     store = pltpu.make_async_copy(staged, out_hbm.at[0, :, :, pl.ds(column, n)], out_sem)
     store.start()
     store.wait()
 
 
-def last_block(sink, source, got_b, got_d, out):
+def last_block(sink, source, got2, out):
     n = sink.shape[0]
     return pl.pallas_call(
         last_kernel,
@@ -459,7 +443,6 @@
             pl.BlockSpec((2 * n, 2 * n), lambda i: (0, 0)),
             HBM,
             HBM,
-            HBM,
         ],
         out_specs=HBM,
         scratch_shapes=[
@@ -469,10 +452,14 @@
             pltpu.SemaphoreType.DMA,
         ],
         out_shape=jax.ShapeDtypeStruct(out.shape, out.dtype),
-        input_output_aliases={4: 0},
+        input_output_aliases={3: 0},
         compiler_params=pltpu.CompilerParams(vmem_limit_bytes=40 * 1024 * 1024),
         name="last",
-    )(sink, source, got_b, got_d, out)
+    )(sink, source, got2, out)
+
+
+def xor_pairs(count, bit):
+    return [(i, i ^ bit) for i in range(count)]
 
 
 def block_body(eigenvectors, perambulator, momenta, ratios, source_slice):
@@ -483,6 +470,7 @@
     n = eigenvectors.shape[4]
     quarter = n // 4
     spins = lax.axis_size("space")
+    times = lax.axis_size("tm")
     j = lax.axis_index("space")
     inner = (j == 1) | (j == 2)
     odd = lax.axis_index("tm") % 2
@@ -492,21 +480,16 @@
         return lax.ppermute(value, axis, pairs)
 
     middle = [(1, 2), (2, 1)]
-    ends = [(0, 3), (3, 0)]
     inward = [(0, 1), (3, 2)]
     outward = [(1, 0), (2, 3)]
-    skip_in = [(0, 2), (3, 1)]
-    skip_out = [(1, 3), (2, 0)]
-    core = [(0, 1), (1, 0), (2, 3), (3, 2)]
-    chip = [(0, 2), (2, 0), (1, 3), (3, 1)]
+    core = xor_pairs(times, 1)
+    chip = xor_pairs(times, 2)
 
     by3, by1, by2 = pick_blocks(tau)
-    got_a = move(by3, middle)
-    got_n = move(by1, inward + outward)
-    got_c = move(by2, skip_out)
+    got3 = move(by3, xor_pairs(spins, 3))
+    got1 = move(by1, xor_pairs(spins, 1))
+    got2 = move(by2, xor_pairs(spins, 2))
     rounded_a, rounded_b, full_a, full_b = elemental_sums(eigenvectors[0], momenta, ratios)
-    got_b = move(by2, skip_in)
-    got_d = move(by3, ends)
 
     pieces = []
     for rounded, full in ((rounded_a, full_a), (rounded_b, full_b)):
@@ -524,8 +507,8 @@
         pieces.append((sink, here, far, beside))
     pieces = [piece for pair in zip(*pieces) for piece in pair]
 
-    out, sink, source = three_blocks(source_slice, pieces, tau, (got_n, got_a, got_c), spins)
-    return last_block(sink, source, got_b, got_d, out)
+    out, sink, source = three_blocks(source_slice, pieces, tau, [in_hbm(got) for got in (got1, got3)], spins)
+    return last_block(sink, source, got2, out)
 
 
 def fits(mesh, eigenvectors, perambulator):

time: 112 us -> 101 us (0.902)
  waiting for transfers between devices: 66.8 us -> 60.1 us
  starting transfers between devices: 23.5 us -> 19.1 us
    ppermute x17 -> x15, waiting for transfers between devices: 66.8 us -> 60.1 us  [move(): return lax.ppermute(value, axis, pairs)]
    ppermute x17 -> x15, starting transfers between devices: 23.5 us -> 19.1 us  [move(): return lax.ppermute(value, axis, pairs)]
  transfers between devices with their start and end apart: 17 -> 15, of which waited for: 8 -> 8; matrix products, arithmetic and copies ran while one was open for 1% -> 2% of each run, Pallas kernels for 7% -> 7%
where the time goes in v1:
time: 101 us
  waiting for transfers between devices  60.1 us (60%)
  starting transfers between devices  19.1 us (19%)
  Pallas kernels  18 us (18%)
  other arithmetic  2.42 us (2%)
  between operations  1.05 us (1%)
    ppermute x15, waiting for transfers between devices, move(): return lax.ppermute(value, axis, pairs)  60.1 us
    ppermute x15, starting transfers between devices, move(): return lax.ppermute(value, axis, pairs)  19.1 us
    pallas_call x1, Pallas kernels, elemental_sums(): pl.pallas_call(elemental_kernel, grid=(1,), in_specs=[HBM] * 3, out_specs...  8.23 us
    pallas_call x1, Pallas kernels, three_blocks(): pl.pallas_call(three_kernel, grid_spec=pltpu.PrefetchScalarGridSpec(num_s...  5.09 us
    pallas_call x1, Pallas kernels, last_block(): pl.pallas_call(last_kernel, grid=(1,), in_specs=[pl.BlockSpec((n, 2 * n),...  2.35 us
    pallas_call x1, Pallas kernels, pick_blocks(): pl.pallas_call(pick_kernel, in_specs=[HBM], out_specs=[HBM] * 3, scratch_...  2.34 us
  transfers between devices with their start and end apart: 15, of which 8 were waited for; matrix products, arithmetic and copies ran while one was open for 2% of the time, Pallas kernels for 7%

profile of v1, /device:TPU:0, one launch (start us, length us, event | category | flops | bytes accessed | tf_op | source)
XLA Modules:
  0.0 100.7 jit_solution(16014014946039347008)
XLA Ops:
  0.0 8.2 %elementals.1 = (bf16[2,192,384]{2,1,0:T(8,128)(2,1)S(1)}, bf16[2,192,384]{2,1,0:T(8,128)(2,1)S(1)}, f32[2,192,384]{2,1,0:T(8,128)S(1)}, f32[2,192,384]{2,1,0:T(8,128)S(1)}) custom-call(s32[2,3]{1,0:T(2,128)} %momenta_hbm.1, s32[2,2]{1,0:T(2,128)} %ratios_hbm.1, bf16[2,3,768,384]{3,2,1,0:T(8,128)(2,1)} %bitcast.8), custom_call_target="tpu_custom_call" | custom-call | tf_op jit(solution)/shard_map/elementals/pallas_call | solution.py:295
  8.2 5.0 %collective-permute-start = (bf16[2,192,384]{2,1,0:T(8,128)(2,1)S(1)}, bf16[2,192,384]{2,1,0:T(8,128)(2,1)S(1)}, u32[]{:S(2)}, u32[]{:S(2)}) collective-permute-start(bf16[2,192,384]{2,1,0:T(8,128)(2,1)S(1)} %get-tuple-element.16), channel_id=1, source_target_pairs={{0,4},{12,8},{1,5},{13,9},{2,6},{14,10},{3,7},{15,11},{16,20},{28,... | collective-permute-start | bytes 884744 | tf_op jit(solution)/shard_map/ppermute | solution.py:480
  13.2 1.3 %collective-permute-start.3 = (bf16[2,192,384]{2,1,0:T(8,128)(2,1)S(1)}, bf16[2,192,384]{2,1,0:T(8,128)(2,1)S(1)}, u32[]{:S(2)}, u32[]{:S(2)}) collective-permute-start(bf16[2,192,384]{2,1,0:T(8,128)(2,1)S(1)} %get-tuple-element.18), channel_id=1, source_target_pairs={{0,4},{12,8},{1,5},{13,9},{2,6},{14,10},{3,7},{15,11},{16,20},{28,... | collective-permute-start | bytes 884744 | tf_op jit(solution)/shard_map/ppermute | solution.py:480
  14.5 6.0 %collective-permute-done = bf16[2,192,384]{2,1,0:T(8,128)(2,1)S(1)} collective-permute-done((bf16[2,192,384]{2,1,0:T(8,128)(2,1)S(1)}, bf16[2,192,384]{2,1,0:T(8,128)(2,1)S(1)}, u32[]{:S(2)}, u32[]{:S(2)}) %collective-permute-start) | collective-permute-done | bytes 294944 | tf_op jit(solution)/shard_map/ppermute | solution.py:480
  20.6 0.1 fusion
  20.6 0.7 collective-permute-start.1
  21.3 4.4 %collective-permute-done.3 = bf16[2,192,384]{2,1,0:T(8,128)(2,1)S(1)} collective-permute-done((bf16[2,192,384]{2,1,0:T(8,128)(2,1)S(1)}, bf16[2,192,384]{2,1,0:T(8,128)(2,1)S(1)}, u32[]{:S(2)}, u32[]{:S(2)}) %collective-permute-start.3) | collective-permute-done | bytes 294944 | tf_op jit(solution)/shard_map/ppermute | solution.py:480
  25.8 0.7 collective-permute-start.4
  26.5 0.1 add_convert_fusion.1
  26.6 1.3 %collective-permute-start.2 = (bf16[2,192,384]{2,1,0:T(8,128)(2,1)S(1)}, bf16[2,192,384]{2,1,0:T(8,128)(2,1)}, u32[]{:S(2)}, u32[]{:S(2)}) collective-permute-start(bf16[2,192,384]{2,1,0:T(8,128)(2,1)S(1)} %add_convert_fusion.1), channel_id=1, source_target_pairs={{4,0},{8,12},{5,1},{9,13},{6,2},{10,14},{7,3},{11,15},{20,16},{24,... | collective-permute-start | bytes 884744 | tf_op jit(solution)/shard_map/ppermute | solution.py:480
  28.0 0.1 add_convert_fusion
  28.1 1.6 %collective-permute-start.5 = (bf16[2,192,384]{2,1,0:T(8,128)(2,1)S(1)}, bf16[2,192,384]{2,1,0:T(8,128)(2,1)}, u32[]{:S(2)}, u32[]{:S(2)}) collective-permute-start(bf16[2,192,384]{2,1,0:T(8,128)(2,1)S(1)} %add_convert_fusion), channel_id=1, source_target_pairs={{4,0},{8,12},{5,1},{9,13},{6,2},{10,14},{7,3},{11,15},{20,16},{24,... | collective-permute-start | bytes 884744 | tf_op jit(solution)/shard_map/ppermute | solution.py:480
  29.7 10.0 %collective-permute-done.2 = bf16[2,192,384]{2,1,0:T(8,128)(2,1)} collective-permute-done((bf16[2,192,384]{2,1,0:T(8,128)(2,1)S(1)}, bf16[2,192,384]{2,1,0:T(8,128)(2,1)}, u32[]{:S(2)}, u32[]{:S(2)}) %collective-permute-start.2) | collective-permute-done | bytes 294944 | tf_op jit(solution)/shard_map/ppermute | solution.py:480
  39.6 1.0 broadcast_select_fusion.3.refs_0_
  40.7 0.1 collective-permute-start.6
  40.7 2.3 %pick.1 = (bf16[2,384,384]{2,1,0:T(8,128)(2,1)}, bf16[2,384,384]{2,1,0:T(8,128)(2,1)}, bf16[2,384,384]{2,1,0:T(8,128)(2,1)}) custom-call(bf16[2,4,384,384]{3,2,1,0:T(8,128)(2,1)} %bitcast.6), custom_call_target="tpu_custom_call" | custom-call | tf_op jit(solution)/shard_map/pick/pallas_call | solution.py:173
  43.1 0.1 collective-permute-start.12
  43.2 2.2 %collective-permute-start.13 = (bf16[2,384,384]{2,1,0:T(8,128)(2,1)}, bf16[2,384,384]{2,1,0:T(8,128)(2,1)}, u32[]{:S(2)}, u32[]{:S(2)}) collective-permute-start(bf16[2,384,384]{2,1,0:T(8,128)(2,1)} %get-tuple-element.20), channel_id=1, source_target_pairs={{0,12},{4,8},{8,4},{12,0},{1,13},{5,9},{9,5},{13,1},{2,14},{6,10},... | collective-permute-start | bytes 1769480 | tf_op jit(solution)/shard_map/ppermute | solution.py:480
  45.4 1.3 %collective-permute-start.14 = (bf16[2,384,384]{2,1,0:T(8,128)(2,1)}, bf16[2,384,384]{2,1,0:T(8,128)(2,1)S(1)}, u32[]{:S(2)}, u32[]{:S(2)}) collective-permute-start(bf16[2,384,384]{2,1,0:T(8,128)(2,1)} %get-tuple-element.23), channel_id=1, source_target_pairs={{0,8},{4,12},{8,0},{12,4},{1,9},{5,13},{9,1},{13,5},{2,10},{6,14},... | collective-permute-start | bytes 1769480 | tf_op jit(solution)/shard_map/ppermute | solution.py:480
  47.3 1.0 %broadcast_select_fusion.2.refs_1_ = bf16[2,192,384]{2,1,0:T(8,128)(2,1)S(1)} fusion(bf16[2,192,384]{2,1,0:T(8,128)(2,1)S(1)} %add_convert_fusion, bf16[2,192,384]{2,1,0:T(8,128)(2,1)} %collective-permute-done.5, pred[]{:T(512)S(6)} %or.3), kind=kLoop, calls=%fused_computation.8 | loop fusion | flops 147456 | bytes 884737 | tf_op jit(solution)/shard_map/jit(_where)/select_n | solution.py:501
  48.3 0.1 collective-permute-start.7
  48.5 1.6 %collective-permute-start.8 = (bf16[2,96,384]{2,1,0:T(8,128)(2,1)S(1)}, bf16[2,96,384]{2,1,0:T(8,128)(2,1)S(1)}, u32[]{:S(2)}, u32[]{:S(2)}) collective-permute-start(bf16[2,96,384]{2,1,0:T(8,128)(2,1)S(1)} %constant_dynamic-slice_fusion.1), channel_id=1, source_target_pairs={{0,2},{1,3},{2,0},{3,1},{4,6},{5,7},{6,4},{7,5},{8,10},{9,11},{10,... | collective-permute-start | bytes 442376 | tf_op jit(solution)/shard_map/ppermute | solution.py:480
  50.2 1.5 %collective-permute-start.9 = (bf16[2,96,384]{2,1,0:T(8,128)(2,1)S(1)}, bf16[2,96,384]{2,1,0:T(8,128)(2,1)S(1)}, u32[]{:S(2)}, u32[]{:S(2)}) collective-permute-start(bf16[2,96,384]{2,1,0:T(8,128)(2,1)S(1)} %constant_dynamic-slice_fusion), channel_id=1, source_target_pairs={{0,2},{1,3},{2,0},{3,1},{4,6},{5,7},{6,4},{7,5},{8,10},{9,11},{10,... | collective-permute-start | bytes 442376 | tf_op jit(solution)/shard_map/ppermute | solution.py:480
  51.6 3.2 %collective-permute-done.8.refs_4_ = bf16[2,96,384]{2,1,0:T(8,128)(2,1)S(1)} collective-permute-done((bf16[2,96,384]{2,1,0:T(8,128)(2,1)S(1)}, bf16[2,96,384]{2,1,0:T(8,128)(2,1)S(1)}, u32[]{:S(2)}, u32[]{:S(2)}) %collective-permute-start.8) | collective-permute-done | bytes 147488 | tf_op jit(solution)/shard_map/ppermute | solution.py:480
  54.8 1.1 %collective-permute-start.10 = (bf16[2,96,384]{2,1,0:T(8,128)(2,1)S(1)}, bf16[2,96,384]{2,1,0:T(8,128)(2,1)S(1)}, u32[]{:S(2)}, u32[]{:S(2)}) collective-permute-start(bf16[2,96,384]{2,1,0:T(8,128)(2,1)S(1)} %collective-permute-done.8.refs_4_), channel_id=1, source_target_pairs={{0,1},{1,0},{2,3},{3,2},{4,5},{5,4},{6,7},{7,6},{8,9},{9,8},{10,11... | collective-permute-start | bytes 442376 | tf_op jit(solution)/shard_map/ppermute | solution.py:480
  56.0 2.0 %collective-permute-done.9.refs_5_ = bf16[2,96,384]{2,1,0:T(8,128)(2,1)S(1)} collective-permute-done((bf16[2,96,384]{2,1,0:T(8,128)(2,1)S(1)}, bf16[2,96,384]{2,1,0:T(8,128)(2,1)S(1)}, u32[]{:S(2)}, u32[]{:S(2)}) %collective-permute-start.9) | collective-permute-done | bytes 147488 | tf_op jit(solution)/shard_map/ppermute | solution.py:480
  58.0 0.7 collective-permute-start.11
  58.7 0.8 collective-permute-done.12.refs_9_
  59.5 13.1 %collective-permute-done.13.refs_10_ = bf16[2,384,384]{2,1,0:T(8,128)(2,1)} collective-permute-done((bf16[2,384,384]{2,1,0:T(8,128)(2,1)}, bf16[2,384,384]{2,1,0:T(8,128)(2,1)}, u32[]{:S(2)}, u32[]{:S(2)}) %collective-permute-start.13) | collective-permute-done | bytes 589856 | tf_op jit(solution)/shard_map/ppermute | solution.py:480
  72.6 5.1 %three.1 = (f32[1,2,384,1536]{3,2,1,0:T(8,128)}, bf16[384,768]{1,0:T(8,128)(2,1)S(1)}, bf16[768,768]{1,0:T(8,128)(2,1)S(1)}) custom-call(s32[1]{0:T(128)} %copy.8.source_slice, bf16[2,192,384]{2,1,0:T(8,128)(2,1)S(1)} %broadcast_select_fusion.3.refs_0_, bf16[2,192,384]{2,1,0:T(8,128)(2,1)S(1)} %broadcast_select_fusion.2.refs_1_, ...), custom_call_target="tpu_custom_call" | custom-call | tf_op jit(solution)/shard_map/three/pallas_call | solution.py:392
  77.7 20.5 %collective-permute-done.14.got2 = bf16[2,384,384]{2,1,0:T(8,128)(2,1)S(1)} collective-permute-done((bf16[2,384,384]{2,1,0:T(8,128)(2,1)}, bf16[2,384,384]{2,1,0:T(8,128)(2,1)S(1)}, u32[]{:S(2)}, u32[]{:S(2)}) %collective-permute-start.14) | collective-permute-done | bytes 589856 | tf_op jit(solution)/shard_map/ppermute | solution.py:480
  98.2 2.3 %last.1 = f32[1,2,384,1536]{3,2,1,0:T(8,128)} custom-call(bf16[384,768]{1,0:T(8,128)(2,1)S(1)} %get-tuple-element.21.sink, bf16[768,768]{1,0:T(8,128)(2,1)S(1)} %get-tuple-element.22.source, bf16[2,384,384]{2,1,0:T(8,128)(2,1)S(1)} %collective-permute-done.14.got2, f32[1,2,384,1536]{3,2,1,0:T(8,128)} %get-tuple-element.24._), custom_call_target="tpu_custom_call", output_to_operand_aliasing={{}: (3, {})} | custom-call | tf_op jit(solution)/shard_map/last/pallas_call | solution.py:438
  (14 shorter events, 0.2 us)
Async XLA Ops:
  8.2 12.3 %collective-permute-start = (bf16[2,192,384]{2,1,0:T(8,128)(2,1)S(1)}, bf16[2,192,384]{2,1,0:T(8,128)(2,1)S(1)}, u32[]{:S(2)}, u32[]{:S(2)}) collective-permute-start(bf16[2,192,384]{2,1,0:T(8,128)(2,1)S(1)} %get-tuple-element.16), channel_id=1, source_target_pairs={{0,4},{12,8},{1,5},{13,9},{2,6},{14,10},{3,7},{15,11},{16,20},{28,... | collective-permute-start | bytes 884744 | tf_op jit(solution)/shard_map/ppermute | solution.py:480
  13.2 12.6 %collective-permute-start.3 = (bf16[2,192,384]{2,1,0:T(8,128)(2,1)S(1)}, bf16[2,192,384]{2,1,0:T(8,128)(2,1)S(1)}, u32[]{:S(2)}, u32[]{:S(2)}) collective-permute-start(bf16[2,192,384]{2,1,0:T(8,128)(2,1)S(1)} %get-tuple-element.18), channel_id=1, source_target_pairs={{0,4},{12,8},{1,5},{13,9},{2,6},{14,10},{3,7},{15,11},{16,20},{28,... | collective-permute-start | bytes 884744 | tf_op jit(solution)/shard_map/ppermute | solution.py:480
  20.6 5.9 %collective-permute-start.1 = (bf16[2,192,384]{2,1,0:T(8,128)(2,1)S(1)}, bf16[2,192,384]{2,1,0:T(8,128)(2,1)S(1)}, u32[]{:S(2)}, u32[]{:S(2)}) collective-permute-start(bf16[2,192,384]{2,1,0:T(8,128)(2,1)S(1)} %fusion), channel_id=1, source_target_pairs={{4,8},{8,4},{5,9},{9,5},{6,10},{10,6},{7,11},{11,7},{20,24},{24,20... | collective-permute-start | bytes 884744 | tf_op jit(solution)/shard_map/ppermute | solution.py:480
  25.8 2.1 %collective-permute-start.4 = (bf16[2,192,384]{2,1,0:T(8,128)(2,1)S(1)}, bf16[2,192,384]{2,1,0:T(8,128)(2,1)S(1)}, u32[]{:S(2)}, u32[]{:S(2)}) collective-permute-start(bf16[2,192,384]{2,1,0:T(8,128)(2,1)S(1)} %fusion.1), channel_id=1, source_target_pairs={{4,8},{8,4},{5,9},{9,5},{6,10},{10,6},{7,11},{11,7},{20,24},{24,20... | collective-permute-start | bytes 884744 | tf_op jit(solution)/shard_map/ppermute | solution.py:480
  26.6 13.0 %collective-permute-start.2 = (bf16[2,192,384]{2,1,0:T(8,128)(2,1)S(1)}, bf16[2,192,384]{2,1,0:T(8,128)(2,1)}, u32[]{:S(2)}, u32[]{:S(2)}) collective-permute-start(bf16[2,192,384]{2,1,0:T(8,128)(2,1)S(1)} %add_convert_fusion.1), channel_id=1, source_target_pairs={{4,0},{8,12},{5,1},{9,13},{6,2},{10,14},{7,3},{11,15},{20,16},{24,... | collective-permute-start | bytes 884744 | tf_op jit(solution)/shard_map/ppermute | solution.py:480
  28.1 44.6 %copy-start = (bf16[1,2,1536,384]{3,2,1,0:T(8,128)(2,1)S(1)}, bf16[1,2,1536,384]{3,2,1,0:T(8,128)(2,1)}, u32[]{:S(2)}) copy-start(bf16[1,2,1536,384]{3,2,1,0:T(8,128)(2,1)} %param.6) | copy-start | bytes 7077892
  28.1 19.2 %collective-permute-start.5 = (bf16[2,192,384]{2,1,0:T(8,128)(2,1)S(1)}, bf16[2,192,384]{2,1,0:T(8,128)(2,1)}, u32[]{:S(2)}, u32[]{:S(2)}) collective-permute-start(bf16[2,192,384]{2,1,0:T(8,128)(2,1)S(1)} %add_convert_fusion), channel_id=1, source_target_pairs={{4,0},{8,12},{5,1},{9,13},{6,2},{10,14},{7,3},{11,15},{20,16},{24,... | collective-permute-start | bytes 884744 | tf_op jit(solution)/shard_map/ppermute | solution.py:480
  40.7 7.8 %collective-permute-start.6 = (bf16[2,192,384]{2,1,0:T(8,128)(2,1)S(1)}, bf16[2,192,384]{2,1,0:T(8,128)(2,1)}, u32[]{:S(2)}, u32[]{:S(2)}) collective-permute-start(bf16[2,192,384]{2,1,0:T(8,128)(2,1)S(1)} %broadcast_select_fusion.3.refs_0_), channel_id=1, source_target_pairs={{0,1},{1,0},{2,3},{3,2},{4,5},{5,4},{6,7},{7,6},{8,9},{9,8},{10,11... | collective-permute-start | bytes 884744 | tf_op jit(solution)/shard_map/ppermute | solution.py:480
  43.1 16.4 %collective-permute-start.12 = (bf16[2,384,384]{2,1,0:T(8,128)(2,1)}, bf16[2,384,384]{2,1,0:T(8,128)(2,1)}, u32[]{:S(2)}, u32[]{:S(2)}) collective-permute-start(bf16[2,384,384]{2,1,0:T(8,128)(2,1)} %get-tuple-element.19), channel_id=1, source_target_pairs={{0,4},{4,0},{8,12},{12,8},{1,5},{5,1},{9,13},{13,9},{2,6},{6,2},{1... | collective-permute-start | bytes 1769480 | tf_op jit(solution)/shard_map/ppermute | solution.py:480
  43.2 29.4 %collective-permute-start.13 = (bf16[2,384,384]{2,1,0:T(8,128)(2,1)}, bf16[2,384,384]{2,1,0:T(8,128)(2,1)}, u32[]{:S(2)}, u32[]{:S(2)}) collective-permute-start(bf16[2,384,384]{2,1,0:T(8,128)(2,1)} %get-tuple-element.20), channel_id=1, source_target_pairs={{0,12},{4,8},{8,4},{12,0},{1,13},{5,9},{9,5},{13,1},{2,14},{6,10},... | collective-permute-start | bytes 1769480 | tf_op jit(solution)/shard_map/ppermute | solution.py:480
  45.4 52.8 %collective-permute-start.14 = (bf16[2,384,384]{2,1,0:T(8,128)(2,1)}, bf16[2,384,384]{2,1,0:T(8,128)(2,1)S(1)}, u32[]{:S(2)}, u32[]{:S(2)}) collective-permute-start(bf16[2,384,384]{2,1,0:T(8,128)(2,1)} %get-tuple-element.23), channel_id=1, source_target_pairs={{0,8},{4,12},{8,0},{12,4},{1,9},{5,13},{9,1},{13,5},{2,10},{6,14},... | collective-permute-start | bytes 1769480 | tf_op jit(solution)/shard_map/ppermute | solution.py:480
  48.3 1.7 %collective-permute-start.7 = (bf16[2,192,384]{2,1,0:T(8,128)(2,1)S(1)}, bf16[2,192,384]{2,1,0:T(8,128)(2,1)S(1)}, u32[]{:S(2)}, u32[]{:S(2)}) collective-permute-start(bf16[2,192,384]{2,1,0:T(8,128)(2,1)S(1)} %broadcast_select_fusion.2.refs_1_), channel_id=1, source_target_pairs={{0,1},{1,0},{2,3},{3,2},{4,5},{5,4},{6,7},{7,6},{8,9},{9,8},{10,11... | collective-permute-start | bytes 884744 | tf_op jit(solution)/shard_map/ppermute | solution.py:480
  48.5 6.3 %collective-permute-start.8 = (bf16[2,96,384]{2,1,0:T(8,128)(2,1)S(1)}, bf16[2,96,384]{2,1,0:T(8,128)(2,1)S(1)}, u32[]{:S(2)}, u32[]{:S(2)}) collective-permute-start(bf16[2,96,384]{2,1,0:T(8,128)(2,1)S(1)} %constant_dynamic-slice_fusion.1), channel_id=1, source_target_pairs={{0,2},{1,3},{2,0},{3,1},{4,6},{5,7},{6,4},{7,5},{8,10},{9,11},{10,... | collective-permute-start | bytes 442376 | tf_op jit(solution)/shard_map/ppermute | solution.py:480
  50.2 7.8 %collective-permute-start.9 = (bf16[2,96,384]{2,1,0:T(8,128)(2,1)S(1)}, bf16[2,96,384]{2,1,0:T(8,128)(2,1)S(1)}, u32[]{:S(2)}, u32[]{:S(2)}) collective-permute-start(bf16[2,96,384]{2,1,0:T(8,128)(2,1)S(1)} %constant_dynamic-slice_fusion), channel_id=1, source_target_pairs={{0,2},{1,3},{2,0},{3,1},{4,6},{5,7},{6,4},{7,5},{8,10},{9,11},{10,... | collective-permute-start | bytes 442376 | tf_op jit(solution)/shard_map/ppermute | solution.py:480
  54.8 17.8 %collective-permute-start.10 = (bf16[2,96,384]{2,1,0:T(8,128)(2,1)S(1)}, bf16[2,96,384]{2,1,0:T(8,128)(2,1)S(1)}, u32[]{:S(2)}, u32[]{:S(2)}) collective-permute-start(bf16[2,96,384]{2,1,0:T(8,128)(2,1)S(1)} %collective-permute-done.8.refs_4_), channel_id=1, source_target_pairs={{0,1},{1,0},{2,3},{3,2},{4,5},{5,4},{6,7},{7,6},{8,9},{9,8},{10,11... | collective-permute-start | bytes 442376 | tf_op jit(solution)/shard_map/ppermute | solution.py:480
  58.0 14.6 %collective-permute-start.11 = (bf16[2,96,384]{2,1,0:T(8,128)(2,1)S(1)}, bf16[2,96,384]{2,1,0:T(8,128)(2,1)S(1)}, u32[]{:S(2)}, u32[]{:S(2)}) collective-permute-start(bf16[2,96,384]{2,1,0:T(8,128)(2,1)S(1)} %collective-permute-done.9.refs_5_), channel_id=1, source_target_pairs={{0,1},{1,0},{2,3},{3,2},{4,5},{5,4},{6,7},{7,6},{8,9},{9,8},{10,11... | collective-permute-start | bytes 442376 | tf_op jit(solution)/shard_map/ppermute | solution.py:480

commit v2 on v1

--- a/solution.py
+++ b/solution.py
@@ -1,3 +1,4 @@
+import functools
 import math
 
 import jax
@@ -10,6 +11,7 @@
 
 LSIDE = 64
 SPINS = 4
+PIECES = 2
 
 
 def spread(value, axis, source):
@@ -152,13 +154,24 @@
     return pltpu.with_memory_space_constraint(array, pltpu.MemorySpace.HBM)
 
 
-def pick_kernel(tau_hbm, by3, by1, by2, buffer, in_sems, out_sems):
+def pick_kernel(distances, tau_hbm, *refs):
+    outs = refs[-3 - len(distances) : -3]
+    buffer, in_sems, out_sems = refs[-3:]
     place = lax.axis_index("space")
+    pieces = in_sems.shape[1]
+    rows = tau_hbm.shape[2] // (pieces // 2)
     loads = []
     stores = []
-    for i, (r, out) in enumerate(((3, by3), (1, by1), (2, by2))):
-        loads.append(pltpu.make_async_copy(tau_hbm.at[:, place ^ r], buffer.at[i], in_sems.at[i]))
-        stores.append(pltpu.make_async_copy(buffer.at[i], out, out_sems.at[i]))
+    for i, out in enumerate(outs):
+        for piece in range(pieces):
+            part = piece % 2
+            some = pl.ds(piece // 2 * rows, rows)
+            source = tau_hbm.at[part, place ^ distances[i], some]
+            kept = buffer.at[i, part, some]
+            loads.append(pltpu.make_async_copy(source, kept, in_sems.at[i, piece]))
+            stores.append(
+                pltpu.make_async_copy(kept, out.at[part, some], out_sems.at[i, piece])
+            )
     for copy in loads:
         copy.start()
     for load, store in zip(loads, stores):
@@ -168,20 +181,22 @@
         copy.wait()
 
 
-def pick_blocks(tau):
+def pick_blocks(tau, distances, after=()):
     _, _, n, columns = tau.shape
+    count = len(distances)
+    pieces = PIECES
     return pl.pallas_call(
-        pick_kernel,
-        in_specs=[HBM],
-        out_specs=[HBM] * 3,
+        functools.partial(pick_kernel, distances),
+        in_specs=[HBM] + [pl.BlockSpec(memory_space=pl.ANY)] * len(after),
+        out_specs=[HBM] * count,
         scratch_shapes=[
-            pltpu.VMEM((3, 2, n, columns), tau.dtype),
-            pltpu.SemaphoreType.DMA((3,)),
-            pltpu.SemaphoreType.DMA((3,)),
-        ],
-        out_shape=[jax.ShapeDtypeStruct((2, n, columns), tau.dtype)] * 3,
+            pltpu.VMEM((count, 2, n, columns), tau.dtype),
+            pltpu.SemaphoreType.DMA((count, pieces)),
+            pltpu.SemaphoreType.DMA((count, pieces)),
+        ],
+        out_shape=[jax.ShapeDtypeStruct((2, n, columns), tau.dtype)] * count,
         name="pick",
-    )(in_hbm(tau))
+    )(in_hbm(tau), *after)
 
 
 def elemental_kernel(
@@ -415,7 +430,7 @@
         ],
         compiler_params=pltpu.CompilerParams(vmem_limit_bytes=40 * 1024 * 1024),
         name="three",
-    )(source_slice, *pieces, tau, *got)
+    )(source_slice, *pieces, in_hbm(tau), *got)
 
 
 def last_kernel(sink, source, got2, _, out_hbm, block, staged, sem, out_sem):
@@ -485,11 +500,12 @@
     core = xor_pairs(times, 1)
     chip = xor_pairs(times, 2)
 
-    by3, by1, by2 = pick_blocks(tau)
+    (by3,) = pick_blocks(tau, (3,))
     got3 = move(by3, xor_pairs(spins, 3))
+    rounded_a, rounded_b, full_a, full_b = elemental_sums(eigenvectors[0], momenta, ratios)
+    by1, by2 = pick_blocks(tau, (1, 2), (rounded_b,))
     got1 = move(by1, xor_pairs(spins, 1))
     got2 = move(by2, xor_pairs(spins, 2))
-    rounded_a, rounded_b, full_a, full_b = elemental_sums(eigenvectors[0], momenta, ratios)
 
     pieces = []
     for rounded, full in ((rounded_a, full_a), (rounded_b, full_b)):

time: 101 us -> 97.9 us (0.969)
  waiting for transfers between devices: 60.1 us -> 56.8 us
  Pallas kernels: 18 us -> 20.3 us
  other arithmetic: 2.42 us -> 0.46 us
    ppermute x15, waiting for transfers between devices: 60.1 us -> 56.8 us  [move(): return lax.ppermute(value, axis, pairs)]
    select_n x2, other arithmetic: 2.01 us -> 0.08 us  [ordered_body(): sink = jnp.where(inner, summed, outside)]
    pallas_call x1 -> x2, Pallas kernels: 2.34 us -> 3.89 us  [pick_blocks(): pl.pallas_call(functools.partial(pick_kernel, distances), in_specs=[HBM]...]
  transfers between devices with their start and end apart: 15 -> 15, of which waited for: 8 -> 8; matrix products, arithmetic and copies ran while one was open for 2% -> 1% of each run, Pallas kernels for 7% -> 10%
where the time goes in v2:
time: 97.9 us; the launch traced here: 97.6 us
  waiting for transfers between devices  56.8 us (58%)
  Pallas kernels  20.3 us (21%)
  starting transfers between devices  18.1 us (18%)
  between operations  1.07 us (1%)
    ppermute x15, waiting for transfers between devices, move(): return lax.ppermute(value, axis, pairs)  56.8 us
    ppermute x15, starting transfers between devices, move(): return lax.ppermute(value, axis, pairs)  18.1 us
    pallas_call x1, Pallas kernels, elemental_sums(): pl.pallas_call(elemental_kernel, grid=(1,), in_specs=[HBM] * 3, out_specs...  8.23 us
    pallas_call x1, Pallas kernels, three_blocks(): pl.pallas_call(three_kernel, grid_spec=pltpu.PrefetchScalarGridSpec(num_s...  5.79 us
    pallas_call x2, Pallas kernels, pick_blocks(): pl.pallas_call(functools.partial(pick_kernel, distances), in_specs=[HBM]...  3.89 us
    pallas_call x1, Pallas kernels, last_block(): pl.pallas_call(last_kernel, grid=(1,), in_specs=[pl.BlockSpec((n, 2 * n),...  2.35 us
  transfers between devices with their start and end apart: 15, of which 8 were waited for; matrix products, arithmetic and copies ran while one was open for 1% of the time, Pallas kernels for 10%

profile of v2, /device:TPU:0, one launch (start us, length us, event | category | flops | bytes accessed | tf_op | source)
XLA Modules:
  0.0 97.6 jit_solution(4219223845680586882)
XLA Ops:
  0.0 8.2 %elementals.1 = (bf16[2,192,384]{2,1,0:T(8,128)(2,1)S(1)}, bf16[2,192,384]{2,1,0:T(8,128)(2,1)S(1)}, f32[2,192,384]{2,1,0:T(8,128)S(1)}, f32[2,192,384]{2,1,0:T(8,128)S(1)}) custom-call(s32[2,3]{1,0:T(2,128)} %momenta_hbm.1, s32[2,2]{1,0:T(2,128)} %ratios_hbm.1, bf16[2,3,768,384]{3,2,1,0:T(8,128)(2,1)} %bitcast.9), custom_call_target="tpu_custom_call" | custom-call | tf_op jit(solution)/shard_map/elementals/pallas_call | solution.py:310
  8.2 5.0 %collective-permute-start = (bf16[2,192,384]{2,1,0:T(8,128)(2,1)S(1)}, bf16[2,192,384]{2,1,0:T(8,128)(2,1)S(1)}, u32[]{:S(2)}, u32[]{:S(2)}) collective-permute-start(bf16[2,192,384]{2,1,0:T(8,128)(2,1)S(1)} %get-tuple-element.15), channel_id=1, source_target_pairs={{0,4},{12,8},{1,5},{13,9},{2,6},{14,10},{3,7},{15,11},{16,20},{28,... | collective-permute-start | bytes 884744 | tf_op jit(solution)/shard_map/ppermute | solution.py:495
  13.2 1.3 %collective-permute-start.3 = (bf16[2,192,384]{2,1,0:T(8,128)(2,1)S(1)}, bf16[2,192,384]{2,1,0:T(8,128)(2,1)S(1)}, u32[]{:S(2)}, u32[]{:S(2)}) collective-permute-start(bf16[2,192,384]{2,1,0:T(8,128)(2,1)S(1)} %get-tuple-element.17.refs_0_), channel_id=1, source_target_pairs={{0,4},{12,8},{1,5},{13,9},{2,6},{14,10},{3,7},{15,11},{16,20},{28,... | collective-permute-start | bytes 884744 | tf_op jit(solution)/shard_map/ppermute | solution.py:495
  14.5 6.0 %collective-permute-done = bf16[2,192,384]{2,1,0:T(8,128)(2,1)S(1)} collective-permute-done((bf16[2,192,384]{2,1,0:T(8,128)(2,1)S(1)}, bf16[2,192,384]{2,1,0:T(8,128)(2,1)S(1)}, u32[]{:S(2)}, u32[]{:S(2)}) %collective-permute-start) | collective-permute-done | bytes 294944 | tf_op jit(solution)/shard_map/ppermute | solution.py:495
  20.6 0.1 fusion
  20.7 0.7 collective-permute-start.1
  21.3 4.4 %collective-permute-done.3 = bf16[2,192,384]{2,1,0:T(8,128)(2,1)S(1)} collective-permute-done((bf16[2,192,384]{2,1,0:T(8,128)(2,1)S(1)}, bf16[2,192,384]{2,1,0:T(8,128)(2,1)S(1)}, u32[]{:S(2)}, u32[]{:S(2)}) %collective-permute-start.3) | collective-permute-done | bytes 294944 | tf_op jit(solution)/shard_map/ppermute | solution.py:495
  25.8 0.1 fusion.1
  25.8 0.7 collective-permute-start.4
  26.5 0.0 collective-permute-done.1
  26.5 0.1 add_convert_fusion.1
  26.6 1.3 %collective-permute-start.2 = (bf16[2,192,384]{2,1,0:T(8,128)(2,1)S(1)}, bf16[2,192,384]{2,1,0:T(8,128)(2,1)S(1)}, u32[]{:S(2)}, u32[]{:S(2)}) collective-permute-start(bf16[2,192,384]{2,1,0:T(8,128)(2,1)S(1)} %add_convert_fusion.1), channel_id=1, source_target_pairs={{4,0},{8,12},{5,1},{9,13},{6,2},{10,14},{7,3},{11,15},{20,16},{24,... | collective-permute-start | bytes 884744 | tf_op jit(solution)/shard_map/ppermute | solution.py:495
  28.0 0.1 add_convert_fusion
  28.1 1.5 %collective-permute-start.5 = (bf16[2,192,384]{2,1,0:T(8,128)(2,1)S(1)}, bf16[2,192,384]{2,1,0:T(8,128)(2,1)S(1)}, u32[]{:S(2)}, u32[]{:S(2)}) collective-permute-start(bf16[2,192,384]{2,1,0:T(8,128)(2,1)S(1)} %add_convert_fusion), channel_id=1, source_target_pairs={{4,0},{8,12},{5,1},{9,13},{6,2},{10,14},{7,3},{11,15},{20,16},{24,... | collective-permute-start | bytes 884744 | tf_op jit(solution)/shard_map/ppermute | solution.py:495
  29.5 10.1 %collective-permute-done.2 = bf16[2,192,384]{2,1,0:T(8,128)(2,1)S(1)} collective-permute-done((bf16[2,192,384]{2,1,0:T(8,128)(2,1)S(1)}, bf16[2,192,384]{2,1,0:T(8,128)(2,1)S(1)}, u32[]{:S(2)}, u32[]{:S(2)}) %collective-permute-start.2) | collective-permute-done | bytes 294944 | tf_op jit(solution)/shard_map/ppermute | solution.py:495
  39.7 0.1 collective-permute-start.6
  39.8 1.9 %pick.3 = bf16[2,384,384]{2,1,0:T(8,128)(2,1)} custom-call(bf16[2,4,384,384]{3,2,1,0:T(8,128)(2,1)} %bitcast.6), custom_call_target="tpu_custom_call" | custom-call | tf_op jit(solution)/shard_map/pick/pallas_call | solution.py:188
  41.7 0.8 collective-permute-start.13
  42.5 2.0 %pick.2 = (bf16[2,384,384]{2,1,0:T(8,128)(2,1)}, bf16[2,384,384]{2,1,0:T(8,128)(2,1)}) custom-call(bf16[2,4,384,384]{3,2,1,0:T(8,128)(2,1)} %bitcast.7, bf16[2,192,384]{2,1,0:T(8,128)(2,1)} %copy-done), custom_call_target="tpu_custom_call" | custom-call | tf_op jit(solution)/shard_map/pick/pallas_call | solution.py:188
  44.5 0.9 collective-permute-start.12
  45.5 2.8 %collective-permute-start.14 = (bf16[2,384,384]{2,1,0:T(8,128)(2,1)}, bf16[2,384,384]{2,1,0:T(8,128)(2,1)S(1)}, u32[]{:S(2)}, u32[]{:S(2)}) collective-permute-start(bf16[2,384,384]{2,1,0:T(8,128)(2,1)} %get-tuple-element.21), channel_id=1, source_target_pairs={{0,8},{4,12},{8,0},{12,4},{1,9},{5,13},{9,1},{13,5},{2,10},{6,14},... | collective-permute-start | bytes 1769480 | tf_op jit(solution)/shard_map/ppermute | solution.py:495
  49.0 0.1 collective-permute-start.7
  49.2 1.6 %collective-permute-start.8 = (bf16[2,96,384]{2,1,0:T(8,128)(2,1)S(1)}, bf16[2,96,384]{2,1,0:T(8,128)(2,1)S(1)}, u32[]{:S(2)}, u32[]{:S(2)}) collective-permute-start(bf16[2,96,384]{2,1,0:T(8,128)(2,1)S(1)} %constant_dynamic-slice_fusion.1), channel_id=1, source_target_pairs={{0,2},{1,3},{2,0},{3,1},{4,6},{5,7},{6,4},{7,5},{8,10},{9,11},{10,... | collective-permute-start | bytes 442376 | tf_op jit(solution)/shard_map/ppermute | solution.py:495
  50.8 1.5 %collective-permute-start.9 = (bf16[2,96,384]{2,1,0:T(8,128)(2,1)S(1)}, bf16[2,96,384]{2,1,0:T(8,128)(2,1)S(1)}, u32[]{:S(2)}, u32[]{:S(2)}) collective-permute-start(bf16[2,96,384]{2,1,0:T(8,128)(2,1)S(1)} %constant_dynamic-slice_fusion), channel_id=1, source_target_pairs={{0,2},{1,3},{2,0},{3,1},{4,6},{5,7},{6,4},{7,5},{8,10},{9,11},{10,... | collective-permute-start | bytes 442376 | tf_op jit(solution)/shard_map/ppermute | solution.py:495
  52.3 3.7 %collective-permute-done.8.refs_4_ = bf16[2,96,384]{2,1,0:T(8,128)(2,1)S(1)} collective-permute-done((bf16[2,96,384]{2,1,0:T(8,128)(2,1)S(1)}, bf16[2,96,384]{2,1,0:T(8,128)(2,1)S(1)}, u32[]{:S(2)}, u32[]{:S(2)}) %collective-permute-start.8) | collective-permute-done | bytes 147488 | tf_op jit(solution)/shard_map/ppermute | solution.py:495
  55.9 2.7 %collective-permute-done.9.refs_5_ = bf16[2,96,384]{2,1,0:T(8,128)(2,1)S(1)} collective-permute-done((bf16[2,96,384]{2,1,0:T(8,128)(2,1)S(1)}, bf16[2,96,384]{2,1,0:T(8,128)(2,1)S(1)}, u32[]{:S(2)}, u32[]{:S(2)}) %collective-permute-start.9) | collective-permute-done | bytes 147488 | tf_op jit(solution)/shard_map/ppermute | solution.py:495
  58.6 1.4 %collective-permute-done.13.refs_10_ = bf16[2,384,384]{2,1,0:T(8,128)(2,1)S(1)} collective-permute-done((bf16[2,384,384]{2,1,0:T(8,128)(2,1)}, bf16[2,384,384]{2,1,0:T(8,128)(2,1)S(1)}, u32[]{:S(2)}, u32[]{:S(2)}) %collective-permute-start.13) | collective-permute-done | bytes 589856 | tf_op jit(solution)/shard_map/ppermute | solution.py:495
  60.1 14.6 %collective-permute-done.12.refs_9_ = bf16[2,384,384]{2,1,0:T(8,128)(2,1)S(1)} collective-permute-done((bf16[2,384,384]{2,1,0:T(8,128)(2,1)}, bf16[2,384,384]{2,1,0:T(8,128)(2,1)S(1)}, u32[]{:S(2)}, u32[]{:S(2)}) %collective-permute-start.12) | collective-permute-done | bytes 589856 | tf_op jit(solution)/shard_map/ppermute | solution.py:495
  74.7 0.8 copy-done.2
  75.5 5.8 %three.1 = (f32[1,2,384,1536]{3,2,1,0:T(8,128)}, bf16[384,768]{1,0:T(8,128)(2,1)S(1)}, bf16[768,768]{1,0:T(8,128)(2,1)S(1)}) custom-call(s32[1]{0:T(128)} %copy.8.source_slice, bf16[2,192,384]{2,1,0:T(8,128)(2,1)S(1)} %broadcast_select_fusion.3.refs_0_, bf16[2,192,384]{2,1,0:T(8,128)(2,1)S(1)} %broadcast_select_fusion.2.refs_1_, ...), custom_call_target="tpu_custom_call" | custom-call | tf_op jit(solution)/shard_map/three/pallas_call | solution.py:407
  81.3 13.8 %collective-permute-done.14.got2 = bf16[2,384,384]{2,1,0:T(8,128)(2,1)S(1)} collective-permute-done((bf16[2,384,384]{2,1,0:T(8,128)(2,1)}, bf16[2,384,384]{2,1,0:T(8,128)(2,1)S(1)}, u32[]{:S(2)}, u32[]{:S(2)}) %collective-permute-start.14) | collective-permute-done | bytes 589856 | tf_op jit(solution)/shard_map/ppermute | solution.py:495
  95.1 2.3 %last.1 = f32[1,2,384,1536]{3,2,1,0:T(8,128)} custom-call(bf16[384,768]{1,0:T(8,128)(2,1)S(1)} %get-tuple-element.19.sink, bf16[768,768]{1,0:T(8,128)(2,1)S(1)} %get-tuple-element.20.source, bf16[2,384,384]{2,1,0:T(8,128)(2,1)S(1)} %collective-permute-done.14.got2, f32[1,2,384,1536]{3,2,1,0:T(8,128)} %get-tuple-element.22._), custom_call_target="tpu_custom_call", output_to_operand_aliasing={{}: (3, {})} | custom-call | tf_op jit(solution)/shard_map/last/pallas_call | solution.py:453
  (19 shorter events, 0.2 us)
Async XLA Ops:
  8.2 33.4 %copy-start = (bf16[2,192,384]{2,1,0:T(8,128)(2,1)}, bf16[2,192,384]{2,1,0:T(8,128)(2,1)S(1)}, u32[]{:S(2)}) copy-start(bf16[2,192,384]{2,1,0:T(8,128)(2,1)S(1)} %get-tuple-element.17.refs_0_) | copy-start | bytes 884740
  8.2 12.3 %collective-permute-start = (bf16[2,192,384]{2,1,0:T(8,128)(2,1)S(1)}, bf16[2,192,384]{2,1,0:T(8,128)(2,1)S(1)}, u32[]{:S(2)}, u32[]{:S(2)}) collective-permute-start(bf16[2,192,384]{2,1,0:T(8,128)(2,1)S(1)} %get-tuple-element.15), channel_id=1, source_target_pairs={{0,4},{12,8},{1,5},{13,9},{2,6},{14,10},{3,7},{15,11},{16,20},{28,... | collective-permute-start | bytes 884744 | tf_op jit(solution)/shard_map/ppermute | solution.py:495
  13.2 12.6 %collective-permute-start.3 = (bf16[2,192,384]{2,1,0:T(8,128)(2,1)S(1)}, bf16[2,192,384]{2,1,0:T(8,128)(2,1)S(1)}, u32[]{:S(2)}, u32[]{:S(2)}) collective-permute-start(bf16[2,192,384]{2,1,0:T(8,128)(2,1)S(1)} %get-tuple-element.17.refs_0_), channel_id=1, source_target_pairs={{0,4},{12,8},{1,5},{13,9},{2,6},{14,10},{3,7},{15,11},{16,20},{28,... | collective-permute-start | bytes 884744 | tf_op jit(solution)/shard_map/ppermute | solution.py:495
  20.7 5.9 %collective-permute-start.1 = (bf16[2,192,384]{2,1,0:T(8,128)(2,1)S(1)}, bf16[2,192,384]{2,1,0:T(8,128)(2,1)S(1)}, u32[]{:S(2)}, u32[]{:S(2)}) collective-permute-start(bf16[2,192,384]{2,1,0:T(8,128)(2,1)S(1)} %fusion), channel_id=1, source_target_pairs={{4,8},{8,4},{5,9},{9,5},{6,10},{10,6},{7,11},{11,7},{20,24},{24,20... | collective-permute-start | bytes 884744 | tf_op jit(solution)/shard_map/ppermute | solution.py:495
  25.8 2.1 %collective-permute-start.4 = (bf16[2,192,384]{2,1,0:T(8,128)(2,1)S(1)}, bf16[2,192,384]{2,1,0:T(8,128)(2,1)S(1)}, u32[]{:S(2)}, u32[]{:S(2)}) collective-permute-start(bf16[2,192,384]{2,1,0:T(8,128)(2,1)S(1)} %fusion.1), channel_id=1, source_target_pairs={{4,8},{8,4},{5,9},{9,5},{6,10},{10,6},{7,11},{11,7},{20,24},{24,20... | collective-permute-start | bytes 884744 | tf_op jit(solution)/shard_map/ppermute | solution.py:495
  26.6 13.1 %collective-permute-start.2 = (bf16[2,192,384]{2,1,0:T(8,128)(2,1)S(1)}, bf16[2,192,384]{2,1,0:T(8,128)(2,1)S(1)}, u32[]{:S(2)}, u32[]{:S(2)}) collective-permute-start(bf16[2,192,384]{2,1,0:T(8,128)(2,1)S(1)} %add_convert_fusion.1), channel_id=1, source_target_pairs={{4,0},{8,12},{5,1},{9,13},{6,2},{10,14},{7,3},{11,15},{20,16},{24,... | collective-permute-start | bytes 884744 | tf_op jit(solution)/shard_map/ppermute | solution.py:495
  28.1 20.9 %collective-permute-start.5 = (bf16[2,192,384]{2,1,0:T(8,128)(2,1)S(1)}, bf16[2,192,384]{2,1,0:T(8,128)(2,1)S(1)}, u32[]{:S(2)}, u32[]{:S(2)}) collective-permute-start(bf16[2,192,384]{2,1,0:T(8,128)(2,1)S(1)} %add_convert_fusion), channel_id=1, source_target_pairs={{4,0},{8,12},{5,1},{9,13},{6,2},{10,14},{7,3},{11,15},{20,16},{24,... | collective-permute-start | bytes 884744 | tf_op jit(solution)/shard_map/ppermute | solution.py:495
  39.7 9.3 %collective-permute-start.6 = (bf16[2,192,384]{2,1,0:T(8,128)(2,1)S(1)}, bf16[2,192,384]{2,1,0:T(8,128)(2,1)S(1)}, u32[]{:S(2)}, u32[]{:S(2)}) collective-permute-start(bf16[2,192,384]{2,1,0:T(8,128)(2,1)S(1)} %broadcast_select_fusion.3.refs_0_), channel_id=1, source_target_pairs={{0,1},{1,0},{2,3},{3,2},{4,5},{5,4},{6,7},{7,6},{8,9},{9,8},{10,11... | collective-permute-start | bytes 884744 | tf_op jit(solution)/shard_map/ppermute | solution.py:495
  41.7 18.4 %collective-permute-start.13 = (bf16[2,384,384]{2,1,0:T(8,128)(2,1)}, bf16[2,384,384]{2,1,0:T(8,128)(2,1)S(1)}, u32[]{:S(2)}, u32[]{:S(2)}) collective-permute-start(bf16[2,384,384]{2,1,0:T(8,128)(2,1)} %pick.3), channel_id=1, source_target_pairs={{0,12},{4,8},{8,4},{12,0},{1,13},{5,9},{9,5},{13,1},{2,14},{6,10},... | collective-permute-start | bytes 1769480 | tf_op jit(solution)/shard_map/ppermute | solution.py:495
  44.5 30.2 %collective-permute-start.12 = (bf16[2,384,384]{2,1,0:T(8,128)(2,1)}, bf16[2,384,384]{2,1,0:T(8,128)(2,1)S(1)}, u32[]{:S(2)}, u32[]{:S(2)}) collective-permute-start(bf16[2,384,384]{2,1,0:T(8,128)(2,1)} %get-tuple-element.18), channel_id=1, source_target_pairs={{0,4},{4,0},{8,12},{12,8},{1,5},{5,1},{9,13},{13,9},{2,6},{6,2},{1... | collective-permute-start | bytes 1769480 | tf_op jit(solution)/shard_map/ppermute | solution.py:495
  45.5 49.6 %collective-permute-start.14 = (bf16[2,384,384]{2,1,0:T(8,128)(2,1)}, bf16[2,384,384]{2,1,0:T(8,128)(2,1)S(1)}, u32[]{:S(2)}, u32[]{:S(2)}) collective-permute-start(bf16[2,384,384]{2,1,0:T(8,128)(2,1)} %get-tuple-element.21), channel_id=1, source_target_pairs={{0,8},{4,12},{8,0},{12,4},{1,9},{5,13},{9,1},{13,5},{2,10},{6,14},... | collective-permute-start | bytes 1769480 | tf_op jit(solution)/shard_map/ppermute | solution.py:495
  49.0 1.7 %collective-permute-start.7 = (bf16[2,192,384]{2,1,0:T(8,128)(2,1)S(1)}, bf16[2,192,384]{2,1,0:T(8,128)(2,1)S(1)}, u32[]{:S(2)}, u32[]{:S(2)}) collective-permute-start(bf16[2,192,384]{2,1,0:T(8,128)(2,1)S(1)} %broadcast_select_fusion.2.refs_1_), channel_id=1, source_target_pairs={{0,1},{1,0},{2,3},{3,2},{4,5},{5,4},{6,7},{7,6},{8,9},{9,8},{10,11... | collective-permute-start | bytes 884744 | tf_op jit(solution)/shard_map/ppermute | solution.py:495
  49.2 6.8 %collective-permute-start.8 = (bf16[2,96,384]{2,1,0:T(8,128)(2,1)S(1)}, bf16[2,96,384]{2,1,0:T(8,128)(2,1)S(1)}, u32[]{:S(2)}, u32[]{:S(2)}) collective-permute-start(bf16[2,96,384]{2,1,0:T(8,128)(2,1)S(1)} %constant_dynamic-slice_fusion.1), channel_id=1, source_target_pairs={{0,2},{1,3},{2,0},{3,1},{4,6},{5,7},{6,4},{7,5},{8,10},{9,11},{10,... | collective-permute-start | bytes 442376 | tf_op jit(solution)/shard_map/ppermute | solution.py:495
  50.8 7.8 %collective-permute-start.9 = (bf16[2,96,384]{2,1,0:T(8,128)(2,1)S(1)}, bf16[2,96,384]{2,1,0:T(8,128)(2,1)S(1)}, u32[]{:S(2)}, u32[]{:S(2)}) collective-permute-start(bf16[2,96,384]{2,1,0:T(8,128)(2,1)S(1)} %constant_dynamic-slice_fusion), channel_id=1, source_target_pairs={{0,2},{1,3},{2,0},{3,1},{4,6},{5,7},{6,4},{7,5},{8,10},{9,11},{10,... | collective-permute-start | bytes 442376 | tf_op jit(solution)/shard_map/ppermute | solution.py:495
  55.9 18.8 %collective-permute-start.10 = (bf16[2,96,384]{2,1,0:T(8,128)(2,1)S(1)}, bf16[2,96,384]{2,1,0:T(8,128)(2,1)S(1)}, u32[]{:S(2)}, u32[]{:S(2)}) collective-permute-start(bf16[2,96,384]{2,1,0:T(8,128)(2,1)S(1)} %collective-permute-done.8.refs_4_), channel_id=1, source_target_pairs={{0,1},{1,0},{2,3},{3,2},{4,5},{5,4},{6,7},{7,6},{8,9},{9,8},{10,11... | collective-permute-start | bytes 442376 | tf_op jit(solution)/shard_map/ppermute | solution.py:495
  58.6 16.1 %collective-permute-start.11 = (bf16[2,96,384]{2,1,0:T(8,128)(2,1)S(1)}, bf16[2,96,384]{2,1,0:T(8,128)(2,1)S(1)}, u32[]{:S(2)}, u32[]{:S(2)}) collective-permute-start(bf16[2,96,384]{2,1,0:T(8,128)(2,1)S(1)} %collective-permute-done.9.refs_5_), channel_id=1, source_target_pairs={{0,1},{1,0},{2,3},{3,2},{4,5},{5,4},{6,7},{7,6},{8,9},{9,8},{10,11... | collective-permute-start | bytes 442376 | tf_op jit(solution)/shard_map/ppermute | solution.py:495
  60.1 14.7 %copy-start.1 = (bf16[2,384,384]{2,1,0:T(8,128)(2,1)}, bf16[2,384,384]{2,1,0:T(8,128)(2,1)S(1)}, u32[]{:S(2)}) copy-start(bf16[2,384,384]{2,1,0:T(8,128)(2,1)S(1)} %collective-permute-done.13.refs_10_) | copy-start | bytes 1769476
  74.7 0.8 copy-start.2
